TPU v7x, 512 devices: a whole 4x8x8 slice. The times are simulated.
512 devices in a mesh: box: 128 (over z, y, core), field: 4 (over x).
Axes of the slice: x: 4, y: 8, z: 8, core: 2. Of those that a mesh axis runs over, the one named last changes fastest.
Arguments:
- incident: bfloat16 [2, 2048, 65536], P(None, 'field', 'box'), may hold values from -6 to 6
- leaf_inverse: bfloat16 [128, 2, 512, 512], P('box', None, 'field'), may hold values from -0.1875 to 0.1875
- contrast: float32 [65536], P('box'), may hold values from 0.2 to 1
- skel_index: int32 [128, 2, 256], replicated, may hold values from 0 to 511
- ranks: int32 [128, 2], replicated, may hold values from 128 to 256, as said below
- top_core: bfloat16 [2, 256, 8192], P(None, None, 'box'), may hold values from -0.25 to 0.25
Outputs:
- total_field: float32 [2, 2048, 65536], P(None, 'field', 'box')
Inputs may be any that keep to these rules, and one draw needn't show every extreme that they name: At each level some box has rank exactly 256; most ranks lie near 256 // 2.
All inputs are finite; a program needn't handle non-finite values.
Results may differ from a plain program's by a relative error of at most 0.0003.
Values may be sent and summed in bfloat16 or wider, within the bound.
A program may use at most 64 MiB of HBM per device.

v0:
```python
import jax
import jax.numpy as jnp
from jax import lax
from jax.sharding import PartitionSpec as P

SIDE = 8


WAVENUM = 0.7
HIGH = lax.Precision.HIGHEST


def laid_out(blocks, dim):
    shape = list(blocks.shape[1:])
    shape[dim] *= blocks.shape[0]
    return jnp.moveaxis(blocks, 0, dim).reshape(shape)


def sent_to_all(shard, axis):
    peers = lax.axis_size(axis)
    return lax.all_to_all(
        jnp.broadcast_to(shard[None], (peers, *shard.shape)), axis, 0, 0, tiled=True
    )


def collect(shard, axis, dim):
    return laid_out(sent_to_all(shard, axis), dim)


def from_partner(value, axis, apart):
    mask = 2**apart
    pairs = [(source, source ^ mask) for source in range(lax.axis_size(axis))]
    return lax.ppermute(value, axis, pairs)


def positions(box_at, index_list):
    px = (SIDE * box_at + index_list % SIDE).astype(jnp.float32)
    py = (index_list // SIDE % SIDE).astype(jnp.float32)
    pz = (index_list // (SIDE * SIDE)).astype(jnp.float32)
    return jnp.stack([px, py, pz])


def selector(index_list, rank_now, width):
    rows = jnp.arange(index_list.shape[0], dtype=jnp.int32)[:, None]
    cols = jnp.arange(width, dtype=jnp.int32)[None, :]
    hit = (index_list[:, None] == cols) & (rows < rank_now)
    return hit.astype(jnp.float32)


def kernel_parts(own_pos, far_pos):
    diff = own_pos[:, :, None] - far_pos[:, None, :]
    dist = jnp.sqrt(jnp.sum(diff * diff, axis=0))
    return (jnp.cos(WAVENUM * dist) / dist, jnp.sin(WAVENUM * dist) / dist)


def complex_apply(mat_re, mat_im, vec):
    out_re = jnp.einsum("km,fm->fk", mat_re, vec[0], precision=HIGH) - jnp.einsum(
        "km,fm->fk", mat_im, vec[1], precision=HIGH
    )
    out_im = jnp.einsum("km,fm->fk", mat_re, vec[1], precision=HIGH) + jnp.einsum(
        "km,fm->fk", mat_im, vec[0], precision=HIGH
    )
    return jnp.stack([out_re, out_im])


def leaf_product(real_in, imag_in, mat_re, mat_im):
    dims = (((1,), (1,)), ((), ()))
    out_re = lax.dot_general(
        real_in, mat_re, dims, preferred_element_type=jnp.float32
    ) - lax.dot_general(imag_in, mat_im, dims, preferred_element_type=jnp.float32)
    out_im = lax.dot_general(
        imag_in, mat_re, dims, preferred_element_type=jnp.float32
    ) + lax.dot_general(real_in, mat_im, dims, preferred_element_type=jnp.float32)
    return jnp.stack([out_re, out_im])


def body(incident, leaf_inverse, contrast, skel_index, ranks, top_core):
    width = incident.shape[2]
    box_at = lax.axis_index("box")
    real_in = incident[0]
    imag_in = incident[1]
    block_rows = collect(leaf_inverse, "field", 2)
    state = leaf_product(real_in, imag_in, block_rows[0, 0], block_rows[0, 1])
    for merge_level in range(2):
        far_at = jnp.bitwise_xor(box_at, 1 << merge_level)
        idx_own = skel_index[box_at, merge_level]
        idx_far = skel_index[far_at, merge_level]
        sel = selector(idx_own, ranks[box_at, merge_level], width)
        skel_vals = jnp.einsum("cfn,kn->cfk", state, sel, precision=HIGH)
        skel_q = jnp.dot(sel, contrast, precision=HIGH)
        far_vals = from_partner(skel_vals * skel_q, "box", merge_level)
        green_re, green_im = kernel_parts(positions(box_at, idx_own), positions(far_at, idx_far))
        pushed = complex_apply(green_re, green_im, far_vals)
        state = state - jnp.einsum("cfk,kn->cfn", pushed, sel, precision=HIGH)
    core_part = top_core
    for core_bit in range(2):
        other_part = from_partner(core_part, "box", core_bit)
        upper = box_at >> core_bit & 1 == 1
        core_part = jnp.where(
            upper,
            jnp.concatenate([other_part, core_part], 2),
            jnp.concatenate([core_part, other_part], 2),
        )
    core_full = core_part.astype(jnp.float32)
    sel_top = selector(skel_index[box_at, 1], ranks[box_at, 1], width)
    coarse = jnp.einsum("cfn,kn->cfk", state, sel_top, precision=HIGH)
    pushed = complex_apply(core_full[0], core_full[1], coarse)
    return state - jnp.einsum("cfk,kn->cfn", pushed, sel_top, precision=HIGH)


def solution(mesh):
    return jax.shard_map(
        body,
        mesh=mesh,
        in_specs=(
            P(None, "field", "box"),
            P("box", None, "field", None),
            P("box"),
            P(),
            P(),
            P(None, None, "box"),
        ),
        out_specs=P(None, "field", "box"),
        check_vma=False,
    )
```

profile of v0, /device:TPU:1, one launch (start us, length us, event | category | flops | bytes accessed | tf_op | source)
XLA Modules:
  0.0 82.3 jit_solution(329139408945235609)
XLA Ops:
  0.0 0.0 copy-start
  0.0 0.0 copy-start.3
  0.0 2.0 %broadcast_in_dim.5 = bf16[4,1,2,128,512]{4,3,2,1,0:T(8,128)(2,1)} broadcast(bf16[2,128,512]{2,1,0:T(8,128)(2,1)} %bitcast.168), dimensions={2,3,4} | broadcast | bytes 1310720 | tf_op jit(solution)/shard_map/broadcast_in_dim | solution.py:22
  2.0 0.0 copy-start.1
  2.0 5.0 %all-to-all-start = ((bf16[4,1,2,128,512]{4,3,2,1,0:T(8,128)(2,1)}), bf16[4,1,2,128,512]{4,3,2,1,0:T(8,128)(2,1)S(1)}, u32[]{:S(2)}, u32[]{:S(2)}) async-start(bf16[4,1,2,128,512]{4,3,2,1,0:T(8,128)(2,1)} %broadcast_in_dim.5), calls=%async_computation | async-start | bytes 2097152 | tf_op jit(solution)/shard_map/all_to_all | solution.py:21
  7.0 0.0 copy-done.3
  7.0 0.6 constant_dynamic-slice_fusion.5
  7.7 0.6 iota_compare_fusion.3
  8.3 0.7 fusion.71
  9.0 0.8 fusion.72
  9.8 0.0 copy-done
  9.8 0.4 fusion.27
  10.3 6.5 %all-to-all-done = bf16[4,1,2,128,512]{4,3,2,1,0:T(8,128)(2,1)S(1)} async-done(((bf16[4,1,2,128,512]{4,3,2,1,0:T(8,128)(2,1)}), bf16[4,1,2,128,512]{4,3,2,1,0:T(8,128)(2,1)S(1)}, u32[]{:S(2)}, u32[]{:S(2)}) %all-to-all-start) | async-done | bytes 1048608 | tf_op jit(solution)/shard_map/all_to_all | solution.py:21
  16.7 0.1 copy.8
  16.8 0.0 copy-done.1
  16.8 0.5 fusion.24
  17.3 0.5 fusion.20
  17.8 0.5 fusion.4
  18.2 0.5 fusion.3
  18.7 1.2 %fusion.2 = f32[2,512,256]{2,1,0:T(8,128)S(1)} fusion(f32[1,512,512]{2,1,0:T(8,128)S(1)} %fusion.3, f32[1,512,512]{2,1,0:T(8,128)S(1)} %fusion.4, f32[256]{0:T(256)S(1)} %bitcast.178, s32[256]{0:T(256)S(1)} %bitcast.175, pred[256]{0:T(512)(128)(4,1)S(1)} %iota_compare_fusion.3), kind=kOutput, calls=%fused_computation.5 | convolution fusion | flops 1611661312 | bytes 3148032 | tf_op jit(solution)/shard_map/cfn,kn->cfk/dot_general | solution.py:89
  19.9 8.7 %collective-permute-start = (f32[2,512,256]{2,1,0:T(8,128)S(1)}, f32[2,512,256]{2,1,0:T(8,128)S(1)}, u32[]{:S(2)}, u32[]{:S(2)}) collective-permute-start(f32[2,512,256]{2,1,0:T(8,128)S(1)} %fusion.2), channel_id=1, source_target_pairs={{0,4},{4,0},{8,12},{12,8},{16,20},{20,16},{24,28},{28,24},{32,36},... | collective-permute-start | bytes 3145736 | tf_op jit(solution)/shard_map/ppermute | solution.py:33
  28.7 0.6 iota_compare_fusion.2
  29.4 0.2 multiply_reduce_fusion.1
  29.5 0.4 fusion.31
  29.9 0.8 collective-permute-done
  30.8 1.5 %fusion.35 = f32[512,256]{1,0:T(8,128)S(1)} fusion(f32[2,512,256]{2,1,0:T(8,128)S(1)} %collective-permute-done, f32[256,256]{1,0:T(8,128)S(1)} %multiply_reduce_fusion.1), kind=kOutput, calls=%fused_computation.57 | convolution fusion | flops 402784256 | bytes 1310720 | tf_op jit(solution)/shard_map/km,fm->fk/dot_general | solution.py:57
  32.3 1.5 %fusion.34 = f32[512,256]{1,0:T(8,128)S(1)} fusion(f32[2,512,256]{2,1,0:T(8,128)S(1)} %collective-permute-done, f32[256,256]{1,0:T(8,128)S(1)} %multiply_reduce_fusion.1), kind=kOutput, calls=%fused_computation.56 | convolution fusion | flops 402784256 | bytes 1310720 | tf_op jit(solution)/shard_map/km,fm->fk/dot_general | solution.py:60
  33.8 1.5 %fusion.10 = f32[1,512,256]{2,1,0:T(8,128)S(1)} fusion(f32[512,256]{1,0:T(8,128)S(1)} %fusion.35, f32[2,512,256]{2,1,0:T(8,128)S(1)} %collective-permute-done, f32[256,256]{1,0:T(8,128)S(1)} %multiply_reduce_fusion.1), kind=kOutput, calls=%fused_computation.22 | convolution fusion | flops 402915328 | bytes 1835008 | tf_op jit(solution)/shard_map/km,fm->fk/dot_general | solution.py:57
  35.4 1.5 %fusion.9 = f32[1,512,256]{2,1,0:T(8,128)S(1)} fusion(f32[512,256]{1,0:T(8,128)S(1)} %fusion.34, f32[2,512,256]{2,1,0:T(8,128)S(1)} %collective-permute-done, f32[256,256]{1,0:T(8,128)S(1)} %multiply_reduce_fusion.1), kind=kOutput, calls=%fused_computation.20 | convolution fusion | flops 402915328 | bytes 1835008 | tf_op jit(solution)/shard_map/km,fm->fk/dot_general | solution.py:60
  36.9 1.2 %fusion = f32[2,512,512]{2,1,0:T(8,128)S(1)} fusion(f32[1,512,512]{2,1,0:T(8,128)S(1)} %fusion.3, f32[1,512,512]{2,1,0:T(8,128)S(1)} %fusion.4, f32[1,512,256]{2,1,0:T(8,128)S(1)} %fusion.9, f32[1,512,256]{2,1,0:T(8,128)S(1)} %fusion.10, s32[256]{0:T(256)S(1)} %bitcast.176, pred[256]{0:T(512)(128)(4,1)S(1)} %iota_compare_fusion.3), kind=kOutput, calls=%fused_computation.1 | convolution fusion | flops 1612185600 | bytes 5244160 | tf_op jit(solution)/shard_map/cfk,kn->cfn/dot_general | solution.py:94
  38.1 0.0 copy-start.2
  38.1 2.2 %convolution_multiply_fusion = f32[2,512,256]{2,1,0:T(8,128)} fusion(f32[2,512,512]{2,1,0:T(8,128)S(1)} %fusion, f32[256]{0:T(256)S(1)} %bitcast.177, s32[256]{0:T(256)S(1)} %bitcast.170, pred[256]{0:T(512)(128)(4,1)S(1)} %iota_compare_fusion.2), kind=kOutput, calls=%fused_computation.6 | convolution fusion | flops 1611137024 | bytes 3148032 | tf_op jit(solution)/shard_map/cfn,kn->cfk/dot_general | solution.py:89
  40.3 2.9 %collective-permute-start.1 = (f32[2,512,256]{2,1,0:T(8,128)}, f32[2,512,256]{2,1,0:T(8,128)S(1)}, u32[]{:S(2)}, u32[]{:S(2)}) collective-permute-start(f32[2,512,256]{2,1,0:T(8,128)} %convolution_multiply_fusion), channel_id=1, source_target_pairs={{0,8},{4,12},{8,0},{12,4},{16,24},{20,28},{24,16},{28,20},{32,40},... | collective-permute-start | bytes 3145736 | tf_op jit(solution)/shard_map/ppermute | solution.py:33
  43.2 0.0 copy-done.2
  43.2 2.6 %collective-permute-start.2 = (bf16[2,256,64]{1,2,0:T(8,128)(2,1)S(1)}, bf16[2,256,64]{1,2,0:T(8,128)(2,1)S(1)}, u32[]{:S(2)}, u32[]{:S(2)}) collective-permute-start(bf16[2,256,64]{1,2,0:T(8,128)(2,1)S(1)} %copy-done.2), channel_id=1, source_target_pairs={{0,4},{4,0},{8,12},{12,8},{16,20},{20,16},{24,28},{28,24},{32,36},... | collective-permute-start | bytes 196616 | tf_op jit(solution)/shard_map/ppermute | solution.py:33
  45.8 0.8 %collective-permute-done.2 = bf16[2,256,64]{1,2,0:T(8,128)(2,1)S(1)} collective-permute-done((bf16[2,256,64]{1,2,0:T(8,128)(2,1)S(1)}, bf16[2,256,64]{1,2,0:T(8,128)(2,1)S(1)}, u32[]{:S(2)}, u32[]{:S(2)}) %collective-permute-start.2) | collective-permute-done | bytes 65568 | tf_op jit(solution)/shard_map/ppermute | solution.py:33
  46.6 2.6 %collective-permute-start.3 = (bf16[2,256,128]{1,2,0:T(8,128)(2,1)S(1)}, bf16[2,256,128]{1,2,0:T(8,128)(2,1)S(1)}, u32[]{:S(2)}, u32[]{:S(2)}) collective-permute-start(bf16[2,256,128]{1,2,0:T(8,128)(2,1)S(1)} %maximum_select_fusion.1), channel_id=1, source_target_pairs={{0,8},{4,12},{8,0},{12,4},{16,24},{20,28},{24,16},{28,20},{32,40},... | collective-permute-start | bytes 393224 | tf_op jit(solution)/shard_map/ppermute | solution.py:33
  49.3 0.2 multiply_reduce_fusion
  49.5 20.0 %collective-permute-done.3 = bf16[2,256,128]{1,2,0:T(8,128)(2,1)S(1)} collective-permute-done((bf16[2,256,128]{1,2,0:T(8,128)(2,1)S(1)}, bf16[2,256,128]{1,2,0:T(8,128)(2,1)S(1)}, u32[]{:S(2)}, u32[]{:S(2)}) %collective-permute-start.3) | collective-permute-done | bytes 131104 | tf_op jit(solution)/shard_map/ppermute | solution.py:33
  69.5 0.1 maximum_select_fusion
  69.6 0.0 collective-permute-done.1
  69.6 1.5 %fusion.37 = f32[512,256]{1,0:T(8,128)S(1)} fusion(f32[2,512,256]{2,1,0:T(8,128)S(1)} %collective-permute-done.1, f32[256,256]{1,0:T(8,128)S(1)} %multiply_reduce_fusion), kind=kOutput, calls=%fused_computation.59 | convolution fusion | flops 402784256 | bytes 1310720 | tf_op jit(solution)/shard_map/km,fm->fk/dot_general | solution.py:57
  71.2 1.5 %fusion.36 = f32[512,256]{1,0:T(8,128)S(1)} fusion(f32[2,512,256]{2,1,0:T(8,128)S(1)} %collective-permute-done.1, f32[256,256]{1,0:T(8,128)S(1)} %multiply_reduce_fusion), kind=kOutput, calls=%fused_computation.58 | convolution fusion | flops 402784256 | bytes 1310720 | tf_op jit(solution)/shard_map/km,fm->fk/dot_general | solution.py:60
  72.7 1.5 %fusion.8 = f32[1,512,256]{2,1,0:T(8,128)S(1)} fusion(f32[512,256]{1,0:T(8,128)S(1)} %fusion.37, f32[2,512,256]{2,1,0:T(8,128)S(1)} %collective-permute-done.1, f32[256,256]{1,0:T(8,128)S(1)} %multiply_reduce_fusion), kind=kOutput, calls=%fused_computation.18 | convolution fusion | flops 402915328 | bytes 1835008 | tf_op jit(solution)/shard_map/km,fm->fk/dot_general | solution.py:57
  74.3 1.5 %fusion.7 = f32[1,512,256]{2,1,0:T(8,128)S(1)} fusion(f32[512,256]{1,0:T(8,128)S(1)} %fusion.36, f32[2,512,256]{2,1,0:T(8,128)S(1)} %collective-permute-done.1, f32[256,256]{1,0:T(8,128)S(1)} %multiply_reduce_fusion), kind=kOutput, calls=%fused_computation.16 | convolution fusion | flops 402915328 | bytes 1835008 | tf_op jit(solution)/shard_map/km,fm->fk/dot_general | solution.py:60
  75.8 1.2 %convolution_subtract_fusion.1 = f32[2,512,512]{2,1,0:T(8,128)S(1)} fusion(f32[2,512,512]{2,1,0:T(8,128)S(1)} %fusion, f32[1,512,256]{2,1,0:T(8,128)S(1)} %fusion.7, f32[1,512,256]{2,1,0:T(8,128)S(1)} %fusion.8, s32[256]{0:T(256)S(1)} %bitcast.171, pred[256]{0:T(512)(128)(4,1)S(1)} %iota_compare_fusion.2), kind=kOutput, calls=%fused_computation.4 | convolution fusion | flops 1611661312 | bytes 5244160 | tf_op jit(solution)/shard_map/cfk,kn->cfn/dot_general | solution.py:94
  77.0 1.2 %fusion.55 = f32[2,512,256]{2,1,0:T(8,128)S(1)} fusion(f32[2,512,512]{2,1,0:T(8,128)S(1)} %convolution_subtract_fusion.1, s32[256]{0:T(256)S(1)} %bitcast.172, pred[256]{0:T(512)(128)(4,1)S(1)} %iota_compare_fusion.2), kind=kOutput, calls=%fused_computation.79 | convolution fusion | flops 1610874880 | bytes 3147008 | tf_op jit(solution)/shard_map/cfn,kn->cfk/dot_general | solution.py:106
  78.2 0.4 fusion.38
  78.6 0.4 fusion.39
  79.0 0.4 fusion.6
  79.4 0.4 fusion.5
  79.8 2.5 %convolution_subtract_fusion = f32[2,512,512]{2,1,0:T(8,128)} fusion(f32[2,512,512]{2,1,0:T(8,128)S(1)} %convolution_subtract_fusion.1, f32[1,512,256]{2,1,0:T(8,128)S(1)} %fusion.5, f32[1,512,256]{2,1,0:T(8,128)S(1)} %fusion.6, s32[256]{0:T(256)S(1)} %bitcast.173, pred[256]{0:T(512)(128)(4,1)S(1)} %iota_compare_fusion.2), kind=kOutput, calls=%fused_computation.3 | convolution fusion | flops 1611661312 | bytes 5244160 | tf_op jit(solution)/shard_map/cfk,kn->cfn/dot_general | solution.py:108
  (5 shorter events, 0.1 us)
Async XLA Ops:
  0.0 9.8 %copy-start = (f32[512]{0:T(512)S(1)}, f32[512]{0:T(512)}, u32[]{:S(2)}) copy-start(f32[512]{0:T(512)} %param.8) | copy-start | bytes 6148
  0.0 7.0 %copy-start.3 = (s32[128,2]{0,1:T(2,128)S(1)}, s32[128,2]{0,1:T(2,128)}, u32[]{:S(2)}) copy-start(s32[128,2]{0,1:T(2,128)} %param.10) | copy-start | bytes 3076
  2.0 14.8 %copy-start.1 = (bf16[2,512,512]{2,1,0:T(8,128)(2,1)S(1)}, bf16[2,512,512]{2,1,0:T(8,128)(2,1)}, u32[]{:S(2)}) copy-start(bf16[2,512,512]{2,1,0:T(8,128)(2,1)} %param.6) | copy-start | bytes 3145732
  2.0 14.7 %all-to-all-start = ((bf16[4,1,2,128,512]{4,3,2,1,0:T(8,128)(2,1)}), bf16[4,1,2,128,512]{4,3,2,1,0:T(8,128)(2,1)S(1)}, u32[]{:S(2)}, u32[]{:S(2)}) async-start(bf16[4,1,2,128,512]{4,3,2,1,0:T(8,128)(2,1)} %broadcast_in_dim.5), calls=%async_computation | async-start | bytes 2097152 | tf_op jit(solution)/shard_map/all_to_all | solution.py:21
  19.9 10.8 %collective-permute-start = (f32[2,512,256]{2,1,0:T(8,128)S(1)}, f32[2,512,256]{2,1,0:T(8,128)S(1)}, u32[]{:S(2)}, u32[]{:S(2)}) collective-permute-start(f32[2,512,256]{2,1,0:T(8,128)S(1)} %fusion.2), channel_id=1, source_target_pairs={{0,4},{4,0},{8,12},{12,8},{16,20},{20,16},{24,28},{28,24},{32,36},... | collective-permute-start | bytes 3145736 | tf_op jit(solution)/shard_map/ppermute | solution.py:33
  38.1 5.1 %copy-start.2 = (bf16[2,256,64]{1,2,0:T(8,128)(2,1)S(1)}, bf16[2,256,64]{1,2,0:T(8,128)(2,1)}, u32[]{:S(2)}) copy-start(bf16[2,256,64]{1,2,0:T(8,128)(2,1)} %param.11) | copy-start | bytes 196612
  40.3 29.3 %collective-permute-start.1 = (f32[2,512,256]{2,1,0:T(8,128)}, f32[2,512,256]{2,1,0:T(8,128)S(1)}, u32[]{:S(2)}, u32[]{:S(2)}) collective-permute-start(f32[2,512,256]{2,1,0:T(8,128)} %convolution_multiply_fusion), channel_id=1, source_target_pairs={{0,8},{4,12},{8,0},{12,4},{16,24},{20,28},{24,16},{28,20},{32,40},... | collective-permute-start | bytes 3145736 | tf_op jit(solution)/shard_map/ppermute | solution.py:33
  43.2 3.4 %collective-permute-start.2 = (bf16[2,256,64]{1,2,0:T(8,128)(2,1)S(1)}, bf16[2,256,64]{1,2,0:T(8,128)(2,1)S(1)}, u32[]{:S(2)}, u32[]{:S(2)}) collective-permute-start(bf16[2,256,64]{1,2,0:T(8,128)(2,1)S(1)} %copy-done.2), channel_id=1, source_target_pairs={{0,4},{4,0},{8,12},{12,8},{16,20},{20,16},{24,28},{28,24},{32,36},... | collective-permute-start | bytes 196616 | tf_op jit(solution)/shard_map/ppermute | solution.py:33
  46.6 22.9 %collective-permute-start.3 = (bf16[2,256,128]{1,2,0:T(8,128)(2,1)S(1)}, bf16[2,256,128]{1,2,0:T(8,128)(2,1)S(1)}, u32[]{:S(2)}, u32[]{:S(2)}) collective-permute-start(bf16[2,256,128]{1,2,0:T(8,128)(2,1)S(1)} %maximum_select_fusion.1), channel_id=1, source_target_pairs={{0,8},{4,12},{8,0},{12,4},{16,24},{20,28},{24,16},{28,20},{32,40},... | collective-permute-start | bytes 393224 | tf_op jit(solution)/shard_map/ppermute | solution.py:33
where the time goes:
time: 82.7 us; the launch traced here: 82.3 us
  waiting for transfers between devices  28.2 us (34%)
  matrix products  25.9 us (31%)
  starting transfers between devices  21.8 us (26%)
  other arithmetic  3.33 us (4%)
  local copies, waits for them, and re-layouts  2.77 us (3%)
    ppermute x4, waiting for transfers between devices, from_partner(): return lax.ppermute(value, axis, pairs)  21.7 us
    ppermute x4, starting transfers between devices, from_partner(): return lax.ppermute(value, axis, pairs)  16.8 us
    all_to_all x1, waiting for transfers between devices, sent_to_all(): lax.all_to_all(jnp.broadcast_to(shard[None], (peers, *shard.shape)), axis...  6.49 us
    all_to_all x1, starting transfers between devices, sent_to_all(): lax.all_to_all(jnp.broadcast_to(shard[None], (peers, *shard.shape)), axis...  4.96 us
    dot_general x3, matrix products, complex_apply(): jnp.einsum('km,fm->fk', mat_im, vec[1], precision=HIGH)  3.47 us
    dot_general x3, matrix products, complex_apply(): jnp.einsum('km,fm->fk', mat_im, vec[0], precision=HIGH)  3.45 us
    dot_general x3, matrix products, complex_apply(): jnp.einsum('km,fm->fk', mat_re, vec[0], precision=HIGH)  3.43 us
    dot_general x3, matrix products, complex_apply(): jnp.einsum('km,fm->fk', mat_re, vec[1], precision=HIGH)  3.43 us
  transfers between devices with their start and end apart: 5, of which 4 were waited for; matrix products, arithmetic and copies ran while one was open for 6% of the time, Pallas kernels for 0%

commit v1 on v0

v1 whole, which is shorter than its diff:
```python
import functools

import jax
import jax.numpy as jnp
from jax import lax
from jax.experimental import pallas as pl
from jax.experimental.pallas import tpu as pltpu
from jax.sharding import PartitionSpec as P

MESH = pl.DeviceIdType.MESH
WAVENUM = 0.7
F32 = jnp.float32
BF16 = jnp.bfloat16
CHUNK = 128
TOP = 32767.0


def dot_nn(lhs, rhs):
    return lax.dot_general(lhs, rhs, (((1,), (0,)), ((), ())), preferred_element_type=F32)


def dot_nt(lhs, rhs):
    return lax.dot_general(lhs, rhs, (((1,), (1,)), ((), ())), preferred_element_type=F32)


def halves(value):
    high = value.astype(BF16)
    low = (value - high.astype(F32)).astype(BF16)
    return high, low


def grid_of(index):
    return index & 7, (index >> 3) & 7, index >> 6


def green(far_col, own_row, apart):
    fx, fy, fz = grid_of(far_col)
    ox, oy, oz = grid_of(own_row)
    dx = (fx - ox + apart).astype(F32)
    dy = (fy - oy).astype(F32)
    dz = (fz - oz).astype(F32)
    dist = jnp.sqrt(dx * dx + dy * dy + dz * dz)
    turn = WAVENUM * dist
    inverse = 1.0 / dist
    return jnp.cos(turn) * inverse, jnp.sin(turn) * inverse


def put_complex(ref, re, im):
    half = re.shape[0]
    ref[:half, :half] = re
    ref[:half, half:] = im
    ref[half:, :half] = -im
    ref[half:, half:] = re


def kernel(
    inc, leaf, con, skel, rank_in, core, out,
    x, a, idx, rank, cont, cq, et, es0, es1, g0h, g0l, g1h, g1l, cc,
    ws, wr, cs, cr, ss, sr, v, held,
    lsem, xsend, xrecv, csend, crecv, wsend, wrecv, ksend, krecv, ssend, srecv,
):
    fields, leafs = inc.shape[1], inc.shape[2]
    kmax = skel.shape[2]
    rows = leaf.shape[2]
    box = lax.axis_index("box")
    me = lax.axis_index("field")
    right, left, across = (me + 1) % 4, (me + 3) % 4, (me + 2) % 4
    box1 = box + 1 - 2 * (box % 2)
    box2 = box + 2 - 4 * ((box // 2) % 2)
    box3 = box2 + 1 - 2 * (box % 2)
    quad = box % 4

    def local(src, dst, at):
        copy = pltpu.make_async_copy(src, dst, lsem.at[at])
        copy.start()
        return copy

    load_idx = [
        local(skel.at[who], idx.at[at], at) for at, who in enumerate((box, box1, box2))
    ]
    load_rank = local(rank_in, rank, 3)
    load_con = local(con, cont, 4)
    load_x = local(inc, x, 5)
    load_a = local(leaf.at[0], a.at[me], 6)
    load_c = local(core, cq.at[quad], 7)

    barrier = pltpu.get_barrier_semaphore()
    for peer in ((box, right), (box, left), (box1, me), (box2, me), (box3, me)):
        pl.semaphore_signal(barrier, inc=1, device_id=peer, device_id_type=MESH)
    pl.semaphore_wait(barrier, 5)

    def remote(src, dst, send, recv, peer):
        copy = pltpu.make_async_remote_copy(
            src_ref=src, dst_ref=dst, send_sem=send, recv_sem=recv,
            device_id=peer, device_id_type=MESH,
        )
        copy.start()
        return copy

    def ring(src, owner, part, at, to):
        return remote(src, a.at[owner, part], xsend.at[at], xrecv.at[at], (box, to))

    from_left_re = ring(leaf.at[0, 0], me, 0, 0, right)
    from_right_im = ring(leaf.at[0, 1], me, 1, 3, left)
    from_left_im = ring(leaf.at[0, 1], me, 1, 1, right)
    from_right_re = ring(leaf.at[0, 0], me, 0, 4, left)
    cores = [
        remote(core, cq.at[quad], csend.at[at], crecv.at[at], (who, me))
        for at, who in enumerate((box1, box2, box3))
    ]

    for copy in load_idx:
        copy.wait()
    load_rank.wait()
    load_con.wait()
    own = idx[0]
    own0, own1 = own[0:1], own[1:2]
    far0, far1 = idx[1][0:1], idx[2][1:2]
    at_box = lax.broadcasted_iota(jnp.int32, rank.shape, 1) == box
    ranks = jnp.sum(jnp.where(at_box, rank[...].astype(F32), 0.0), axis=1, keepdims=True)
    at_k = lax.broadcasted_iota(jnp.int32, (1, kmax), 1)
    in0 = at_k.astype(F32) < ranks[0:1]
    in1 = at_k.astype(F32) < ranks[1:2]
    pick0 = jnp.where(in0, own0, -1)
    pick1 = jnp.where(in1, own1, -1)
    pick1_too = jnp.where(in1, own1, -2)
    table = jnp.concatenate([pick0, pick1, far0, far1, own0, own0, own0, own0], axis=0)
    columns = jnp.transpose(table.astype(F32)).astype(jnp.int32)

    both = jnp.concatenate([pick0, pick1], axis=1)
    at_n = lax.broadcasted_iota(jnp.int32, (rows, 2 * kmax), 0)
    contrast = cont[...]
    c_high = contrast.astype(BF16).astype(F32)
    c_mid = (contrast - c_high).astype(BF16).astype(F32)
    c_low = contrast - c_high - c_mid
    zero = jnp.zeros((5, leafs), F32)
    c_rows = jnp.concatenate([c_high, c_mid, c_low, zero], axis=0).astype(BF16)
    weight = jnp.zeros((8, 2 * kmax), F32)
    for block in range(leafs // rows):
        hit = jnp.where(at_n + block * rows == both, 1.0, 0.0).astype(BF16)
        et[block, :rows] = hit
        et[block, rows:] = hit
        weight = weight + dot_nn(c_rows[:, block * rows : (block + 1) * rows], hit)
    weight = jnp.sum(weight, axis=0, keepdims=True)
    q0, q1 = weight[:, :kmax], weight[:, kmax:]

    def block_of(owner, start, size, first):
        matrix = a[owner].reshape(2 * rows, leafs)
        at_f = pl.ds(start, size)
        by_re = dot_nt(x[0, at_f, :], matrix)
        by_im = dot_nt(x[1, at_f, :], matrix)
        y_re = by_re[:, :rows] - by_im[:, rows:]
        y_im = by_re[:, rows:] + by_im[:, :rows]
        at_cols = pl.ds(pl.multiple_of(owner * rows, rows), rows)
        out[0, at_f, at_cols] = y_re
        out[1, at_f, at_cols] = y_im
        high, low = halves(jnp.concatenate([y_re, y_im], axis=0))
        picked = dot_nn(jnp.concatenate([high, low], axis=1), et[owner])
        if not first:
            picked = picked + jnp.concatenate([v[0, at_f, :], v[1, at_f, :]], axis=0)
        v[0, at_f, :] = picked[:size]
        v[1, at_f, :] = picked[size:]

    def whole_block(owner, first):
        for start in range(0, fields, 2 * CHUNK):
            block_of(owner, start, 2 * CHUNK, first)

    load_x.wait()
    load_a.wait()
    whole_block(me, True)

    g_re, g_im = green(columns[:, 2:3], own0, 8 * (box1 - box))
    re_h, re_l = halves(g_re)
    im_h, im_l = halves(g_im)
    put_complex(g0h, re_h, im_h)
    put_complex(g0l, re_l, im_l)

    from_left_re.wait_recv()
    on_right = ring(a.at[left, 0], left, 0, 2, right)
    from_right_im.wait_recv()
    on_left = ring(a.at[right, 1], right, 1, 5, left)

    at_l = lax.broadcasted_iota(jnp.int32, (1, leafs), 1)
    lanes = jnp.concatenate([at_l, pick1_too], axis=1)
    es0[...] = jnp.where(columns[:, 0:1] == lanes, 1.0, 0.0).astype(BF16)
    es1[...] = jnp.where(columns[:, 1:2] == lanes, 1.0, 0.0).astype(BF16)

    from_left_im.wait_recv()
    whole_block(left, False)
    from_right_re.wait_recv()
    whole_block(right, False)

    g_re, g_im = green(columns[:, 3:4], own1, 8 * (box2 - box))
    re_h, re_l = halves(g_re)
    im_h, im_l = halves(g_im)
    put_complex(g1h, re_h, im_h)
    put_complex(g1l, re_l, im_l)

    load_c.wait()
    for copy in cores:
        copy.wait_recv()
    c_re = jnp.concatenate([cq[at, 0] for at in range(4)], axis=0)
    c_im = jnp.concatenate([cq[at, 1] for at in range(4)], axis=0)
    put_complex(cc, c_re, c_im)

    def first_stage(c):
        start = c * CHUNK
        at_f = pl.ds(start, CHUNK)
        block_of(across, start, CHUNK, False)
        value = jnp.concatenate([v[0, at_f, :kmax] * q0, v[1, at_f, :kmax] * q0], axis=1)
        ws[c, 0], ws[c, 1] = halves(value)
        return remote(ws.at[c], wr.at[c], wsend.at[c], wrecv.at[c], (box1, me))

    def coupled(high, low, ref_h, ref_l):
        main = dot_nn(jnp.concatenate([high, low], axis=0), ref_h[...])
        return main[:CHUNK] + main[CHUNK:] + dot_nn(high, ref_l[...])

    def spread(value, ref):
        high, low = halves(jnp.concatenate([value[:, :kmax], value[:, kmax:]], axis=0))
        both_parts = dot_nn(jnp.concatenate([high, low], axis=0), ref)
        return both_parts[: 2 * CHUNK] + both_parts[2 * CHUNK :]

    def second_stage(c, arriving):
        at_f = pl.ds(c * CHUNK, CHUNK)
        arriving.wait_recv()
        pushed = coupled(wr[c, 0], wr[c, 1], g0h, g0l)
        moved = spread(pushed, es0[...])
        v_re = v[0, at_f, kmax:] - moved[:CHUNK, leafs:]
        v_im = v[1, at_f, kmax:] - moved[CHUNK:, leafs:]
        v[0, at_f, kmax:] = v_re
        v[1, at_f, kmax:] = v_im
        most = jnp.max(jnp.maximum(jnp.abs(v_re), jnp.abs(v_im)), axis=0, keepdims=True)
        scale = TOP / jnp.maximum(most, 1e-30)
        code_re = jnp.round(v_re * scale).astype(jnp.int32).astype(jnp.int16)
        code_im = jnp.round(v_im * scale).astype(jnp.int32).astype(jnp.int16)
        cs[c, :, :kmax] = code_re
        cs[c, :, kmax:] = code_im
        step = jnp.maximum(most, 1e-30) * (1.0 / TOP) * q1
        ss[c] = jnp.broadcast_to(step, (8, kmax))
        codes = remote(cs.at[c], cr.at[c], ksend.at[c], krecv.at[c], (box2, me))
        steps = remote(ss.at[c], sr.at[c], ssend.at[c], srecv.at[c], (box2, me))
        out[0, at_f, :] = out[0, at_f, :] - moved[:CHUNK, :leafs]
        out[1, at_f, :] = out[1, at_f, :] - moved[CHUNK:, :leafs]
        return codes, steps

    def third_stage(c, codes, steps):
        at_f = pl.ds(c * CHUNK, CHUNK)
        codes.wait_recv()
        steps.wait_recv()
        step = sr[c][0:1]
        step = jnp.concatenate([step, step], axis=1)
        high, low = halves(cr[c].astype(jnp.int32).astype(F32) * step)
        pushed = coupled(high, low, g1h, g1l)
        held[...] = pushed
        again = spread(pushed, es1[:, leafs:])
        coarse = jnp.concatenate(
            [v[0, at_f, kmax:] - again[:CHUNK], v[1, at_f, kmax:] - again[CHUNK:]], axis=1
        )
        high, low = halves(coarse)
        main = dot_nn(jnp.concatenate([high, low], axis=0), cc[...])
        total = held[...] + (main[:CHUNK] + main[CHUNK:])
        moved = spread(total, es1[:, :leafs])
        out[0, at_f, :] = out[0, at_f, :] - moved[:CHUNK]
        out[1, at_f, :] = out[1, at_f, :] - moved[CHUNK:]

    on_right.wait_recv()
    on_left.wait_recv()
    chunks = fields // CHUNK
    sent = []
    codes = []
    for c in range(chunks + 1):
        if c < chunks:
            sent.append(first_stage(c))
        if c > 0:
            codes.append(second_stage(c - 1, sent[c - 1]))
    for c in range(chunks):
        third_stage(c, *codes[c])

    for copy in (from_left_re, from_left_im, from_right_im, from_right_re, on_right, on_left):
        copy.wait_send()
    for copy in cores + sent:
        copy.wait_send()
    for pair in codes:
        for copy in pair:
            copy.wait_send()


def body(incident, leaf_inverse, contrast, skel_index, ranks, top_core):
    _, fields, leafs = incident.shape
    rows = leaf_inverse.shape[2]
    kmax = skel_index.shape[2]
    boxes, kq = ranks.shape[0], top_core.shape[2]
    chunks = fields // CHUNK
    wide = 2 * kmax
    dma = pltpu.SemaphoreType.DMA
    return pl.pallas_call(
        kernel,
        out_shape=jax.ShapeDtypeStruct(incident.shape, F32),
        in_specs=[pl.BlockSpec(memory_space=pltpu.HBM)] * 6,
        out_specs=pl.BlockSpec(memory_space=pltpu.VMEM),
        scratch_shapes=[
            pltpu.VMEM((2, fields, leafs), BF16),
            pltpu.VMEM((4, 2, rows, leafs), BF16),
            pltpu.VMEM((3, 2, kmax), jnp.int32),
            pltpu.VMEM((2, boxes), jnp.int32),
            pltpu.VMEM((1, leafs), F32),
            pltpu.VMEM((4, 2, kq, kmax), BF16),
            pltpu.VMEM((4, 2 * rows, wide), BF16),
            pltpu.VMEM((kmax, leafs + kmax), BF16),
            pltpu.VMEM((kmax, leafs + kmax), BF16),
            pltpu.VMEM((wide, wide), BF16),
            pltpu.VMEM((wide, wide), BF16),
            pltpu.VMEM((wide, wide), BF16),
            pltpu.VMEM((wide, wide), BF16),
            pltpu.VMEM((wide, wide), BF16),
            pltpu.VMEM((chunks, 2, CHUNK, wide), BF16),
            pltpu.VMEM((chunks, 2, CHUNK, wide), BF16),
            pltpu.VMEM((chunks, CHUNK, wide), jnp.int16),
            pltpu.VMEM((chunks, CHUNK, wide), jnp.int16),
            pltpu.VMEM((chunks, 8, kmax), F32),
            pltpu.VMEM((chunks, 8, kmax), F32),
            pltpu.VMEM((2, fields, wide), F32),
            pltpu.VMEM((CHUNK, wide), F32),
            dma((8,)), dma((6,)), dma((6,)), dma((3,)), dma((3,)),
            dma((chunks,)), dma((chunks,)), dma((chunks,)), dma((chunks,)),
            dma((chunks,)), dma((chunks,)),
        ],
        compiler_params=pltpu.CompilerParams(
            collective_id=0, has_side_effects=True, vmem_limit_bytes=48 << 20
        ),
        name="solve",
    )(
        incident,
        leaf_inverse,
        contrast.reshape(1, leafs),
        skel_index,
        ranks.T,
        jnp.swapaxes(top_core, 1, 2),
    )


def solution(mesh):
    return jax.shard_map(
        body,
        mesh=mesh,
        in_specs=(
            P(None, "field", "box"),
            P("box", None, "field", None),
            P("box"),
            P(),
            P(),
            P(None, None, "box"),
        ),
        out_specs=P(None, "field", "box"),
        check_vma=False,
    )
```

time: 82.7 us -> 42.5 us (0.51)
  Pallas kernels: 0 us -> 35.3 us
  waiting for transfers between devices: 28.2 us -> 0 us
  matrix products: 25.9 us -> 0 us
  starting transfers between devices: 21.8 us -> 0 us
  local copies, waits for them, and re-layouts: 2.77 us -> 6.64 us
  other arithmetic: 3.33 us -> 0 us
    pallas_call x0 -> x1, Pallas kernels: none -> 35.3 us  [body(): pl.pallas_call(kernel, out_shape=jax.ShapeDtypeStruct(incident.shape, F32...]
    dot_general x24 -> x0, matrix products: 25.9 us -> none  [the longest x3 3.47 us: complex_apply(): jnp.einsum('km,fm->fk', mat_im, vec[1], precision=HIGH)]
    ppermute x4 -> x0, waiting for transfers between devices: 21.7 us -> none  [from_partner(): return lax.ppermute(value, axis, pairs)]
    ppermute x4 -> x0, starting transfers between devices: 16.8 us -> none  [from_partner(): return lax.ppermute(value, axis, pairs)]
    unnamed x8 -> x13, local copies, waits for them, and re-layouts: 0.02 us -> 6.64 us
    all_to_all x1 -> x0, waiting for transfers between devices: 6.49 us -> none  [sent_to_all(): lax.all_to_all(jnp.broadcast_to(shard[None], (peers, *shard.shape)), axis...]
    all_to_all x1 -> x0, starting transfers between devices: 4.96 us -> none  [sent_to_all(): lax.all_to_all(jnp.broadcast_to(shard[None], (peers, *shard.shape)), axis...]
    broadcast_in_dim x1 -> x0, local copies, waits for them, and re-layouts: 2.04 us -> none  [sent_to_all(): jnp.broadcast_to(shard[None], (peers, *shard.shape))]
  transfers between devices with their start and end apart: 5 -> 0, of which waited for: 4 -> 0; matrix products, arithmetic and copies ran while one was open for 6% -> 0% of each run, Pallas kernels for 0% -> 0%
where the time goes in v1:
time: 42.5 us; the launch traced here: 41.9 us
  Pallas kernels  35.3 us (83%)
  local copies, waits for them, and re-layouts  6.64 us (16%)
    pallas_call x1, Pallas kernels, body(): pl.pallas_call(kernel, out_shape=jax.ShapeDtypeStruct(incident.shape, F32...  35.3 us
    unnamed x13, local copies, waits for them, and re-layouts  6.64 us

profile of v1, /device:TPU:1, one launch (start us, length us, event | category | flops | bytes accessed | tf_op | source)
XLA Modules:
  0.0 41.9 jit_solution(2826612792764301279)
XLA Ops:
  0.0 0.0 copy-start
  0.0 1.2 %copy-done = bf16[2,512,512]{2,1,0:T(8,128)(2,1)S(1)} copy-done((bf16[2,512,512]{2,1,0:T(8,128)(2,1)S(1)}, bf16[2,512,512]{2,1,0:T(8,128)(2,1)}, u32[]{:S(2)}) %copy-start) | copy-done | bytes 1048600
  1.2 0.0 copy-start.1
  1.2 0.9 %copy-done.1 = bf16[1,2,128,512]{3,2,1,0:T(8,128)(2,1)S(1)} copy-done((bf16[1,2,128,512]{3,2,1,0:T(8,128)(2,1)S(1)}, bf16[1,2,128,512]{3,2,1,0:T(8,128)(2,1)}, u32[]{:S(2)}) %copy-start.1) | copy-done | bytes 262168
  2.2 0.0 copy-start.2
  2.2 0.9 %copy-done.2 = s32[128,2,256]{2,1,0:T(2,128)S(1)} copy-done((s32[128,2,256]{2,1,0:T(2,128)S(1)}, s32[128,2,256]{2,1,0:T(2,128)}, u32[]{:S(2)}) %copy-start.2) | copy-done | bytes 262168
  3.1 0.0 copy-start.3
  3.1 0.8 %copy-done.3 = bf16[2,256,64]{1,2,0:T(8,128)(2,1)S(1)} copy-done((bf16[2,256,64]{1,2,0:T(8,128)(2,1)S(1)}, bf16[2,256,64]{1,2,0:T(8,128)(2,1)}, u32[]{:S(2)}) %copy-start.3) | copy-done | bytes 65560
  4.0 0.0 copy-start.4
  4.0 0.7 %copy-done.4 = f32[512]{0:T(512)S(1)} copy-done((f32[512]{0:T(512)S(1)}, f32[512]{0:T(512)}, u32[]{:S(2)}) %copy-start.4) | copy-done | bytes 2072
  4.6 0.0 copy-start.5
  4.7 0.7 %copy-done.5 = s32[128,2]{0,1:T(2,128)S(1)} copy-done((s32[128,2]{0,1:T(2,128)S(1)}, s32[128,2]{0,1:T(2,128)}, u32[]{:S(2)}) %copy-start.5) | copy-done | bytes 1048
  5.3 35.3 %solve.1 = f32[2,512,512]{2,1,0:T(8,128)S(1)} custom-call(bf16[2,512,512]{2,1,0:T(8,128)(2,1)S(1)} %copy-done, bf16[1,2,128,512]{3,2,1,0:T(8,128)(2,1)S(1)} %copy-done.1, f32[1,512]{1,0:T(1,128)S(1)} %bitcast.4, s32[128,2,256]{2,1,0:T(2,128)S(1)} %copy-done.2, s32[2,128]{1,0:T(2,128)S(1)} %bitcast.5, bf16[2,64,256]{2,1,0:T(8,128)(2,1)S(1)} %bitcast.3), custom_call_target="tpu_custom_call" | custom-call | tf_op jit(solution)/shard_map/solve/pallas_call | solution.py:296
  40.6 1.3 %copy.8 = f32[2,512,512]{2,1,0:T(8,128)} copy(f32[2,512,512]{2,1,0:T(8,128)S(1)} %solve.1) | data formatting | bytes 4194304
Async XLA Ops:
  0.0 1.2 %copy-start = (bf16[2,512,512]{2,1,0:T(8,128)(2,1)S(1)}, bf16[2,512,512]{2,1,0:T(8,128)(2,1)}, u32[]{:S(2)}) copy-start(bf16[2,512,512]{2,1,0:T(8,128)(2,1)} %inc.1) | copy-start | bytes 3145732
  1.2 0.9 %copy-start.1 = (bf16[1,2,128,512]{3,2,1,0:T(8,128)(2,1)S(1)}, bf16[1,2,128,512]{3,2,1,0:T(8,128)(2,1)}, u32[]{:S(2)}) copy-start(bf16[1,2,128,512]{3,2,1,0:T(8,128)(2,1)} %leaf.1) | copy-start | bytes 786436
  2.2 0.9 %copy-start.2 = (s32[128,2,256]{2,1,0:T(2,128)S(1)}, s32[128,2,256]{2,1,0:T(2,128)}, u32[]{:S(2)}) copy-start(s32[128,2,256]{2,1,0:T(2,128)} %skel.1) | copy-start | bytes 786436
  3.1 0.8 %copy-start.3 = (bf16[2,256,64]{1,2,0:T(8,128)(2,1)S(1)}, bf16[2,256,64]{1,2,0:T(8,128)(2,1)}, u32[]{:S(2)}) copy-start(bf16[2,256,64]{1,2,0:T(8,128)(2,1)} %param.11) | copy-start | bytes 196612
  4.0 0.7 %copy-start.4 = (f32[512]{0:T(512)S(1)}, f32[512]{0:T(512)}, u32[]{:S(2)}) copy-start(f32[512]{0:T(512)} %param.8) | copy-start | bytes 6148
  4.6 0.7 %copy-start.5 = (s32[128,2]{0,1:T(2,128)S(1)}, s32[128,2]{0,1:T(2,128)}, u32[]{:S(2)}) copy-start(s32[128,2]{0,1:T(2,128)} %param.10) | copy-start | bytes 3076

commit v2 on v1

--- a/solution.py
+++ b/solution.py
@@ -330,12 +330,17 @@
         ),
         name="solve",
     )(
-        incident,
-        leaf_inverse,
-        contrast.reshape(1, leafs),
-        skel_index,
-        ranks.T,
-        jnp.swapaxes(top_core, 1, 2),
+        *(
+            pltpu.with_memory_space_constraint(value, pltpu.HBM)
+            for value in (
+                incident,
+                leaf_inverse,
+                contrast.reshape(1, leafs),
+                skel_index,
+                ranks.T,
+                jnp.swapaxes(top_core, 1, 2),
+            )
+        )
     )
 
 

time: 42.5 us -> 37.1 us (0.87)
  local copies, waits for them, and re-layouts: 6.64 us -> 1.32 us
    unnamed x13 -> x1, local copies, waits for them, and re-layouts: 6.64 us -> 1.32 us
where the time goes in v2:
time: 37.1 us; the launch traced here: 36.6 us
  Pallas kernels  35.3 us (95%)
  local copies, waits for them, and re-layouts  1.32 us (4%)
    pallas_call x1, Pallas kernels, body(): pl.pallas_call(kernel, out_shape=jax.ShapeDtypeStruct(incident.shape, F32...  35.3 us
    unnamed x1, local copies, waits for them, and re-layouts  1.32 us

profile of v2, /device:TPU:1, one launch (start us, length us, event | category | flops | bytes accessed | tf_op | source)
XLA Modules:
  0.0 36.6 jit_solution(16945050025805831972)
XLA Ops:
  0.0 35.3 %solve.1 = f32[2,512,512]{2,1,0:T(8,128)S(1)} custom-call(bf16[2,512,512]{2,1,0:T(8,128)(2,1)} %inc.1, bf16[1,2,128,512]{3,2,1,0:T(8,128)(2,1)} %leaf.1, f32[1,512]{1,0:T(1,128)} %bitcast.4, s32[128,2,256]{2,1,0:T(2,128)} %skel.1, s32[2,128]{1,0:T(2,128)} %bitcast.5, bf16[2,64,256]{2,1,0:T(8,128)(2,1)} %bitcast.3), custom_call_target="tpu_custom_call" | custom-call | tf_op jit(solution)/shard_map/solve/pallas_call | solution.py:296
  35.3 1.3 %copy.8 = f32[2,512,512]{2,1,0:T(8,128)} copy(f32[2,512,512]{2,1,0:T(8,128)S(1)} %solve.1) | data formatting | bytes 4194304

commit v3 on v1

v3 whole, which is shorter than its diff:
```python
import functools

import jax
import jax.numpy as jnp
from jax import lax
from jax.experimental import pallas as pl
from jax.experimental.pallas import tpu as pltpu
from jax.sharding import PartitionSpec as P

MESH = pl.DeviceIdType.MESH
WAVENUM = 0.7
F32 = jnp.float32
BF16 = jnp.bfloat16
CHUNKS = (64, 128, 128, 128, 64)
TOP = 32767.0


def dot_nn(lhs, rhs):
    return lax.dot_general(lhs, rhs, (((1,), (0,)), ((), ())), preferred_element_type=F32)


def dot_nt(lhs, rhs):
    return lax.dot_general(lhs, rhs, (((1,), (1,)), ((), ())), preferred_element_type=F32)


def halves(value):
    high = value.astype(BF16)
    low = (value - high.astype(F32)).astype(BF16)
    return high, low


def grid_of(index):
    return index & 7, (index >> 3) & 7, index >> 6


def green(far_col, own_row, apart):
    fx, fy, fz = grid_of(far_col)
    ox, oy, oz = grid_of(own_row)
    dx = (fx - ox + apart).astype(F32)
    dy = (fy - oy).astype(F32)
    dz = (fz - oz).astype(F32)
    dist = jnp.sqrt(dx * dx + dy * dy + dz * dz)
    turn = WAVENUM * dist
    inverse = 1.0 / dist
    return jnp.cos(turn) * inverse, jnp.sin(turn) * inverse


def put_complex(ref, re, im):
    half = re.shape[0]
    ref[:half, :half] = re
    ref[:half, half:] = im
    ref[half:, :half] = -im
    ref[half:, half:] = re


def remote(src, dst, send, recv, peer):
    copy = pltpu.make_async_remote_copy(
        src_ref=src, dst_ref=dst, send_sem=send, recv_sem=recv,
        device_id=peer, device_id_type=MESH,
    )
    copy.start()
    return copy


def meet(peers):
    barrier = pltpu.get_barrier_semaphore()
    for peer in peers:
        pl.semaphore_signal(barrier, inc=1, device_id=peer, device_id_type=MESH)
    return barrier


def places():
    box = lax.axis_index("box")
    me = lax.axis_index("field")
    return box, me, box + 1 - 2 * (box % 2), box + 2 - 4 * ((box // 2) % 2)


def leaf_part(x, matrix, picks, at_f):
    rows = matrix.shape[0] // 2
    by_re = dot_nt(x[0, at_f, :], matrix)
    by_im = dot_nt(x[1, at_f, :], matrix)
    y_re = by_re[:, :rows] - by_im[:, rows:]
    y_im = by_re[:, rows:] + by_im[:, :rows]
    high, low = halves(jnp.concatenate([y_re, y_im], axis=0))
    return y_re, y_im, dot_nn(jnp.concatenate([high, low], axis=1), picks)


def gather_kernel(
    inc, leaf, con, skel, rank_in,
    y, v, x, a, et, es0, es1, g0h, g0l, g1h, g1l, weights,
    idx, rank, cont, lsem, xsend, xrecv,
):
    fields, leafs = inc.shape[1], inc.shape[2]
    kmax = skel.shape[2]
    rows = leaf.shape[2]
    box, me, box1, box2 = places()
    right, left = (me + 1) % 4, (me + 3) % 4

    def local(src, dst, at):
        copy = pltpu.make_async_copy(src, dst, lsem.at[at])
        copy.start()
        return copy

    barrier = meet(((box, right), (box, left)))
    load_idx = [
        local(skel.at[who], idx.at[at], at) for at, who in enumerate((box, box1, box2))
    ]
    load_rank = local(rank_in, rank, 3)
    load_con = local(con, cont, 4)
    load_x = local(inc, x, 5)
    load_a = local(leaf.at[0], a.at[me], 6)
    pl.semaphore_wait(barrier, 2)

    def ring(src, owner, part, at, to):
        return remote(src, a.at[owner, part], xsend.at[at], xrecv.at[at], (box, to))

    from_left_re = ring(leaf.at[0, 0], me, 0, 0, right)
    from_right_im = ring(leaf.at[0, 1], me, 1, 3, left)
    from_left_im = ring(leaf.at[0, 1], me, 1, 1, right)
    from_right_re = ring(leaf.at[0, 0], me, 0, 4, left)

    for copy in load_idx:
        copy.wait()
    load_rank.wait()
    load_con.wait()
    own = idx[0]
    own0, own1 = own[0:1], own[1:2]
    far0, far1 = idx[1][0:1], idx[2][1:2]
    at_box = lax.broadcasted_iota(jnp.int32, rank.shape, 1) == box
    ranks = jnp.sum(jnp.where(at_box, rank[...].astype(F32), 0.0), axis=1, keepdims=True)
    at_k = lax.broadcasted_iota(jnp.int32, (1, kmax), 1)
    in0 = at_k.astype(F32) < ranks[0:1]
    in1 = at_k.astype(F32) < ranks[1:2]
    pick0 = jnp.where(in0, own0, -1)
    pick1 = jnp.where(in1, own1, -1)
    pick1_too = jnp.where(in1, own1, -2)
    table = jnp.concatenate([pick0, pick1, far0, far1, own0, own0, own0, own0], axis=0)
    columns = jnp.transpose(table.astype(F32)).astype(jnp.int32)

    both = jnp.concatenate([pick0, pick1], axis=1)
    at_n = lax.broadcasted_iota(jnp.int32, (rows, 2 * kmax), 0)
    contrast = cont[...]
    c_high = contrast.astype(BF16).astype(F32)
    c_mid = (contrast - c_high).astype(BF16).astype(F32)
    c_low = contrast - c_high - c_mid
    zero = jnp.zeros((5, leafs), F32)
    c_rows = jnp.concatenate([c_high, c_mid, c_low, zero], axis=0).astype(BF16)
    weight = jnp.zeros((8, 2 * kmax), F32)
    for block in range(leafs // rows):
        hit = jnp.where(at_n + block * rows == both, 1.0, 0.0).astype(BF16)
        et[block, :rows] = hit
        et[block, rows:] = hit
        weight = weight + dot_nn(c_rows[:, block * rows : (block + 1) * rows], hit)
    weight = jnp.sum(weight, axis=0, keepdims=True)
    weights[...] = jnp.broadcast_to(weight, weights.shape)

    def whole_block(owner, first):
        matrix = a[owner].reshape(2 * rows, leafs)
        size = min(256, fields)
        for start in range(0, fields, size):
            at_f = pl.ds(start, size)
            y_re, y_im, picked = leaf_part(x, matrix, et[owner], at_f)
            at_cols = pl.ds(pl.multiple_of(owner * rows, rows), rows)
            y[0, at_f, at_cols] = y_re
            y[1, at_f, at_cols] = y_im
            if not first:
                picked = picked + jnp.concatenate([v[0, at_f, :], v[1, at_f, :]], axis=0)
            v[0, at_f, :] = picked[:size]
            v[1, at_f, :] = picked[size:]

    load_x.wait()
    load_a.wait()
    whole_block(me, True)

    g_re, g_im = green(columns[:, 2:3], own0, 8 * (box1 - box))
    re_h, re_l = halves(g_re)
    im_h, im_l = halves(g_im)
    put_complex(g0h, re_h, im_h)
    put_complex(g0l, re_l, im_l)

    from_left_re.wait_recv()
    on_right = ring(a.at[left, 0], left, 0, 2, right)
    from_right_im.wait_recv()
    on_left = ring(a.at[right, 1], right, 1, 5, left)

    at_l = lax.broadcasted_iota(jnp.int32, (1, leafs), 1)
    lanes = jnp.concatenate([at_l, pick1_too], axis=1)
    es0[...] = jnp.where(columns[:, 0:1] == lanes, 1.0, 0.0).astype(BF16)
    es1[...] = jnp.where(columns[:, 1:2] == lanes, 1.0, 0.0).astype(BF16)

    from_left_im.wait_recv()
    whole_block(left, False)
    from_right_re.wait_recv()
    whole_block(right, False)

    g_re, g_im = green(columns[:, 3:4], own1, 8 * (box2 - box))
    re_h, re_l = halves(g_re)
    im_h, im_l = halves(g_im)
    put_complex(g1h, re_h, im_h)
    put_complex(g1l, re_l, im_l)

    on_right.wait_recv()
    on_left.wait_recv()
    for copy in (from_left_re, from_left_im, from_right_im, from_right_re, on_right, on_left):
        copy.wait_send()


def merge_kernel(
    y, v_in, x, a, et, es0, es1, g0h, g0l, g1h, g1l, weights, core, out,
    cq, cc, ws, wr, cs, cr, ss, sr, v, held,
    lsem, csend, crecv, wsend, wrecv, ksend, krecv, ssend, srecv,
):
    leafs = y.shape[2]
    kmax = cc.shape[0] // 2
    rows = a.shape[2]
    box, me, box1, box2 = places()
    across = (me + 2) % 4
    quad, quad2 = box % 4, box2 % 4
    barrier = meet(((box1, me), (box2, me)))
    load_c = pltpu.make_async_copy(core, cq.at[quad], lsem)
    load_c.start()
    q0, q1 = weights[0:1, :kmax], weights[0:1, kmax:]
    starts = [sum(CHUNKS[:c]) for c in range(len(CHUNKS))]

    def first_compute(c):
        size = CHUNKS[c]
        at_f = pl.ds(starts[c], size)
        matrix = a[across].reshape(2 * rows, leafs)
        y_re, y_im, picked = leaf_part(x, matrix, et[across], at_f)
        at_cols = pl.ds(pl.multiple_of(across * rows, rows), rows)
        v_re = v_in[0, at_f, :] + picked[:size]
        v_im = v_in[1, at_f, :] + picked[size:]
        v[0, at_f, :] = v_re[:, kmax:]
        v[1, at_f, :] = v_im[:, kmax:]
        value = jnp.concatenate([v_re[:, :kmax] * q0, v_im[:, :kmax] * q0], axis=1)
        ws[0, at_f, :], ws[1, at_f, :] = halves(value)
        out[0, at_f, :] = y[0, at_f, :]
        out[1, at_f, :] = y[1, at_f, :]
        out[0, at_f, at_cols] = y_re
        out[1, at_f, at_cols] = y_im

    def first_send(c):
        at_f = pl.ds(starts[c], CHUNKS[c])
        return remote(ws.at[:, at_f], wr.at[:, at_f], wsend.at[c], wrecv.at[c], (box1, me))

    def coupled(high, low, ref_h, ref_l):
        size = high.shape[0]
        main = dot_nn(jnp.concatenate([high, low], axis=0), ref_h[...])
        return main[:size] + main[size:] + dot_nn(high, ref_l[...])

    def spread(value, matrix):
        size = 2 * value.shape[0]
        high, low = halves(jnp.concatenate([value[:, :kmax], value[:, kmax:]], axis=0))
        parts = dot_nn(jnp.concatenate([high, low], axis=0), matrix)
        return parts[:size] + parts[size:]

    def second_stage(c, arriving):
        size = CHUNKS[c]
        at_f = pl.ds(starts[c], size)
        arriving.wait_recv()
        pushed = coupled(wr[0, at_f, :], wr[1, at_f, :], g0h, g0l)
        moved = spread(pushed, es0[...])
        v_re = v[0, at_f, :] - moved[:size, leafs:]
        v_im = v[1, at_f, :] - moved[size:, leafs:]
        v[0, at_f, :] = v_re
        v[1, at_f, :] = v_im
        most = jnp.max(jnp.maximum(jnp.abs(v_re), jnp.abs(v_im)), axis=0, keepdims=True)
        most = jnp.maximum(most, 1e-30)
        scale = TOP / most
        cs[at_f, :kmax] = jnp.round(v_re * scale).astype(jnp.int32).astype(jnp.int16)
        cs[at_f, kmax:] = jnp.round(v_im * scale).astype(jnp.int32).astype(jnp.int16)
        ss[c] = jnp.broadcast_to(most * (1.0 / TOP) * q1, (8, kmax))
        codes = remote(cs.at[at_f], cr.at[at_f], ksend.at[c], krecv.at[c], (box2, me))
        steps = remote(ss.at[c], sr.at[c], ssend.at[c], srecv.at[c], (box2, me))
        out[0, at_f, :] = out[0, at_f, :] - moved[:size, :leafs]
        out[1, at_f, :] = out[1, at_f, :] - moved[size:, :leafs]
        return codes, steps

    def third_stage(c, codes, steps):
        size = CHUNKS[c]
        at_f = pl.ds(starts[c], size)
        codes.wait_recv()
        steps.wait_recv()
        step = sr[c][0:1]
        step = jnp.concatenate([step, step], axis=1)
        high, low = halves(cr[at_f, :].astype(jnp.int32).astype(F32) * step)
        pushed = coupled(high, low, g1h, g1l)
        held[:size] = pushed
        again = spread(pushed, es1[:, leafs:])
        coarse = jnp.concatenate(
            [v[0, at_f, :] - again[:size], v[1, at_f, :] - again[size:]], axis=1
        )
        high, low = halves(coarse)
        main = dot_nn(jnp.concatenate([high, low], axis=0), cc[...])
        total = held[:size] + (main[:size] + main[size:])
        moved = spread(total, es1[:, :leafs])
        out[0, at_f, :] = out[0, at_f, :] - moved[:size]
        out[1, at_f, :] = out[1, at_f, :] - moved[size:]

    chunks = len(CHUNKS)
    first_compute(0)
    pl.semaphore_wait(barrier, 2)
    sent = [first_send(0)]
    core2 = remote(core, cq.at[quad], csend.at[0], crecv.at[0], (box2, me))
    core1 = remote(core, cq.at[quad], csend.at[1], crecv.at[1], (box1, me))
    codes = []
    for c in range(1, chunks + 1):
        if c < chunks:
            first_compute(c)
            sent.append(first_send(c))
        codes.append(second_stage(c - 1, sent[c - 1]))
        if c == 2:
            core2.wait_recv()
            core3 = remote(cq.at[quad2], cq.at[quad2], csend.at[2], crecv.at[2], (box1, me))

    load_c.wait()
    core1.wait_recv()
    core3.wait_recv()
    c_re = jnp.concatenate([cq[at, 0] for at in range(4)], axis=0)
    c_im = jnp.concatenate([cq[at, 1] for at in range(4)], axis=0)
    put_complex(cc, c_re, c_im)
    for c in range(chunks):
        third_stage(c, *codes[c])

    for copy in [core1, core2, core3] + sent:
        copy.wait_send()
    for pair in codes:
        for copy in pair:
            copy.wait_send()


def body(incident, leaf_inverse, contrast, skel_index, ranks, top_core):
    _, fields, leafs = incident.shape
    rows = leaf_inverse.shape[2]
    kmax = skel_index.shape[2]
    boxes, kq = ranks.shape[0], top_core.shape[2]
    chunks = len(CHUNKS)
    wide = 2 * kmax
    dma = pltpu.SemaphoreType.DMA
    vmem = pl.BlockSpec(memory_space=pltpu.VMEM)
    hbm = pl.BlockSpec(memory_space=pltpu.HBM)
    made = [
        ((2, fields, leafs), F32),
        ((2, fields, wide), F32),
        ((2, fields, leafs), BF16),
        ((4, 2, rows, leafs), BF16),
        ((4, 2 * rows, wide), BF16),
        ((kmax, leafs + kmax), BF16),
        ((kmax, leafs + kmax), BF16),
        ((wide, wide), BF16),
        ((wide, wide), BF16),
        ((wide, wide), BF16),
        ((wide, wide), BF16),
        ((8, wide), F32),
    ]

    def in_hbm(value):
        return pltpu.with_memory_space_constraint(value, pltpu.HBM)

    state = pl.pallas_call(
        gather_kernel,
        out_shape=[jax.ShapeDtypeStruct(*each) for each in made],
        in_specs=[hbm] * 5,
        out_specs=[vmem] * len(made),
        scratch_shapes=[
            pltpu.VMEM((3, 2, kmax), jnp.int32),
            pltpu.VMEM((2, boxes), jnp.int32),
            pltpu.VMEM((1, leafs), F32),
            dma((7,)), dma((6,)), dma((6,)),
        ],
        compiler_params=pltpu.CompilerParams(
            collective_id=0, has_side_effects=True, vmem_limit_bytes=24 << 20
        ),
        name="gather",
    )(*map(in_hbm, (incident, leaf_inverse, contrast.reshape(1, leafs), skel_index, ranks.T)))
    return pl.pallas_call(
        merge_kernel,
        out_shape=jax.ShapeDtypeStruct(incident.shape, F32),
        in_specs=[vmem] * len(made) + [hbm],
        out_specs=vmem,
        scratch_shapes=[
            pltpu.VMEM((4, 2, kq, kmax), BF16),
            pltpu.VMEM((wide, wide), BF16),
            pltpu.VMEM((2, fields, wide), BF16),
            pltpu.VMEM((2, fields, wide), BF16),
            pltpu.VMEM((fields, wide), jnp.int16),
            pltpu.VMEM((fields, wide), jnp.int16),
            pltpu.VMEM((chunks, 8, kmax), F32),
            pltpu.VMEM((chunks, 8, kmax), F32),
            pltpu.VMEM((2, fields, kmax), F32),
            pltpu.VMEM((max(CHUNKS), wide), F32),
            dma, dma((3,)), dma((3,)),
            dma((chunks,)), dma((chunks,)), dma((chunks,)), dma((chunks,)),
            dma((chunks,)), dma((chunks,)),
        ],
        compiler_params=pltpu.CompilerParams(
            collective_id=1, has_side_effects=True, vmem_limit_bytes=28 << 20
        ),
        name="merge",
    )(*state, in_hbm(jnp.swapaxes(top_core, 1, 2)))


def solution(mesh):
    return jax.shard_map(
        body,
        mesh=mesh,
        in_specs=(
            P(None, "field", "box"),
            P("box", None, "field", None),
            P("box"),
            P(),
            P(),
            P(None, None, "box"),
        ),
        out_specs=P(None, "field", "box"),
        check_vma=False,
    )
```

time: 42.5 us -> 38 us (0.89); the launches traced: 41.9 us -> 37.9 us
  local copies, waits for them, and re-layouts: 6.64 us -> 1.32 us
  Pallas kernels: 35.3 us -> 36.6 us
    unnamed x13 -> x1, local copies, waits for them, and re-layouts: 6.64 us -> 1.32 us
    pallas_call x1 -> x2, Pallas kernels: 35.3 us -> 36.6 us  [the longest x1 25 us: body(): pl.pallas_call(merge_kernel, out_shape=jax.ShapeDtypeStruct(incident.shap...]
where the time goes in v3:
time: 38 us; the launch traced here: 37.9 us
  Pallas kernels  36.6 us (96%)
  local copies, waits for them, and re-layouts  1.32 us (3%)
    pallas_call x1, Pallas kernels, body(): pl.pallas_call(merge_kernel, out_shape=jax.ShapeDtypeStruct(incident.shap...  25 us
    pallas_call x1, Pallas kernels, body(): pl.pallas_call(gather_kernel, out_shape=[jax.ShapeDtypeStruct(*each) for...  11.5 us
    unnamed x1, local copies, waits for them, and re-layouts  1.32 us

profile of v3, /device:TPU:1, one launch (start us, length us, event | category | flops | bytes accessed | tf_op | source)
XLA Modules:
  0.0 37.9 jit_solution(434807145361641521)
XLA Ops:
  0.0 11.5 %gather.1 = (f32[2,512,512]{2,1,0:T(8,128)S(1)}, f32[2,512,512]{2,1,0:T(8,128)S(1)}, bf16[2,512,512]{2,1,0:T(8,128)(2,1)S(1)}, bf16[4,2,128,512]{3,2,1,0:T(8,128...) custom-call(bf16[2,512,512]{2,1,0:T(8,128)(2,1)} %inc.1, ...), custom_call_target="tpu_custom_call" | custom-call | tf_op jit(solution)/shard_map/gather/pallas_call | solution.py:360
  11.5 25.0 %merge.1 = f32[2,512,512]{2,1,0:T(8,128)S(1)} custom-call(f32[2,512,512]{2,1,0:T(8,128)S(1)} %get-tuple-element.17.y, f32[2,512,512]{2,1,0:T(8,128)S(1)} %get-tuple-element.18.v_in, bf16[2,512,512]{2,1,0:T(8,128)(2,1)S(1)} %get-tuple-element.19.x, bf16[4,2,128,512]{3,2,1,0:T(8,128)(2,1)S(1)} %get-tuple-element.20.a, ...), custom_call_target="tpu_custom_call" | custom-call | tf_op jit(solution)/shard_map/merge/pallas_call | solution.py:376
  36.6 1.3 %copy.8 = f32[2,512,512]{2,1,0:T(8,128)} copy(f32[2,512,512]{2,1,0:T(8,128)S(1)} %merge.1) | data formatting | bytes 4194304

commit v4 on v3

--- a/solution.py
+++ b/solution.py
@@ -30,19 +30,34 @@
 
 
 def grid_of(index):
-    return index & 7, (index >> 3) & 7, index >> 6
+    return tuple(part.astype(F32) for part in (index & 7, (index >> 3) & 7, index >> 6))
 
 
 def green(far_col, own_row, apart):
     fx, fy, fz = grid_of(far_col)
     ox, oy, oz = grid_of(own_row)
-    dx = (fx - ox + apart).astype(F32)
-    dy = (fy - oy).astype(F32)
-    dz = (fz - oz).astype(F32)
-    dist = jnp.sqrt(dx * dx + dy * dy + dz * dz)
-    turn = WAVENUM * dist
-    inverse = 1.0 / dist
-    return jnp.cos(turn) * inverse, jnp.sin(turn) * inverse
+    dx = fx - (ox - apart)
+    dy = fy - oy
+    dz = fz - oz
+    square = dx * dx + dy * dy + dz * dz
+    inverse = lax.rsqrt(square)
+    inverse = inverse * (1.5 - 0.5 * square * inverse * inverse)
+    turn = WAVENUM * (square * inverse)
+    quarter = jnp.floor(turn * 0.6366197723675814 + 0.5)
+    rest = (turn - quarter * 1.5703125) - quarter * 4.838267948966e-4
+    sq = rest * rest
+    sine = rest + rest * sq * (
+        -1.6666654611e-1 + sq * (8.3321608736e-3 - sq * 1.9515295891e-4)
+    )
+    cosine = 1.0 + sq * (
+        -0.5 + sq * (4.166664568298827e-2 + sq * (-1.388731625493765e-3 + sq * 2.443315711809948e-5))
+    )
+    turns = quarter.astype(jnp.int32)
+    odd = (turns & 1) == 1
+    minus = -inverse
+    re = jnp.where(odd, sine, cosine) * jnp.where(((turns + 1) & 2) == 0, inverse, minus)
+    im = jnp.where(odd, cosine, sine) * jnp.where((turns & 2) == 0, inverse, minus)
+    return re, im
 
 
 def put_complex(ref, re, im):
@@ -172,7 +187,7 @@
     load_a.wait()
     whole_block(me, True)
 
-    g_re, g_im = green(columns[:, 2:3], own0, 8 * (box1 - box))
+    g_re, g_im = green(columns[:, 2:3], own0, (8 * (box1 - box)).astype(F32))
     re_h, re_l = halves(g_re)
     im_h, im_l = halves(g_im)
     put_complex(g0h, re_h, im_h)
@@ -193,7 +208,7 @@
     from_right_re.wait_recv()
     whole_block(right, False)
 
-    g_re, g_im = green(columns[:, 3:4], own1, 8 * (box2 - box))
+    g_re, g_im = green(columns[:, 3:4], own1, (8 * (box2 - box)).astype(F32))
     re_h, re_l = halves(g_re)
     im_h, im_l = halves(g_im)
     put_complex(g1h, re_h, im_h)

time: 38 us -> 37.5 us (0.987)
  Pallas kernels: 36.6 us -> 36 us
where the time goes in v4:
time: 37.5 us; the launch traced here: 37.3 us
  Pallas kernels  36 us (96%)
  local copies, waits for them, and re-layouts  1.32 us (4%)
    pallas_call x1, Pallas kernels, body(): pl.pallas_call(merge_kernel, out_shape=jax.ShapeDtypeStruct(incident.shap...  24.7 us
    pallas_call x1, Pallas kernels, body(): pl.pallas_call(gather_kernel, out_shape=[jax.ShapeDtypeStruct(*each) for...  11.2 us
    unnamed x1, local copies, waits for them, and re-layouts  1.32 us

profile of v4, /device:TPU:1, one launch (start us, length us, event | category | flops | bytes accessed | tf_op | source)
XLA Modules:
  0.0 37.3 jit_solution(7708147799373316581)
XLA Ops:
  0.0 11.2 %gather.1 = (f32[2,512,512]{2,1,0:T(8,128)S(1)}, f32[2,512,512]{2,1,0:T(8,128)S(1)}, bf16[2,512,512]{2,1,0:T(8,128)(2,1)S(1)}, bf16[4,2,128,512]{3,2,1,0:T(8,128...) custom-call(bf16[2,512,512]{2,1,0:T(8,128)(2,1)} %inc.1, ...), custom_call_target="tpu_custom_call" | custom-call | tf_op jit(solution)/shard_map/gather/pallas_call | solution.py:375
  11.2 24.7 %merge.1 = f32[2,512,512]{2,1,0:T(8,128)S(1)} custom-call(f32[2,512,512]{2,1,0:T(8,128)S(1)} %get-tuple-element.17.y, f32[2,512,512]{2,1,0:T(8,128)S(1)} %get-tuple-element.18.v_in, bf16[2,512,512]{2,1,0:T(8,128)(2,1)S(1)} %get-tuple-element.19.x, bf16[4,2,128,512]{3,2,1,0:T(8,128)(2,1)S(1)} %get-tuple-element.20.a, ...), custom_call_target="tpu_custom_call" | custom-call | tf_op jit(solution)/shard_map/merge/pallas_call | solution.py:391
  36.0 1.3 %copy.8 = f32[2,512,512]{2,1,0:T(8,128)} copy(f32[2,512,512]{2,1,0:T(8,128)S(1)} %merge.1) | data formatting | bytes 4194304

commit v5 on v4

--- a/solution.py
+++ b/solution.py
@@ -11,7 +11,7 @@
 WAVENUM = 0.7
 F32 = jnp.float32
 BF16 = jnp.bfloat16
-CHUNKS = (64, 128, 128, 128, 64)
+CHUNKS = (64, 160, 160, 128)
 TOP = 32767.0
 
 
@@ -87,7 +87,9 @@
 def places():
     box = lax.axis_index("box")
     me = lax.axis_index("field")
-    return box, me, box + 1 - 2 * (box % 2), box + 2 - 4 * ((box // 2) % 2)
+    box1 = box + 1 - 2 * (box % 2)
+    box2 = box + 2 - 4 * ((box // 2) % 2)
+    return box, me, box1, box2, box2 + 1 - 2 * (box % 2)
 
 
 def leaf_part(x, matrix, picks, at_f):
@@ -100,23 +102,60 @@
     return y_re, y_im, dot_nn(jnp.concatenate([high, low], axis=1), picks)
 
 
-def gather_kernel(
-    inc, leaf, con, skel, rank_in,
-    y, v, x, a, et, es0, es1, g0h, g0l, g1h, g1l, weights,
-    idx, rank, cont, lsem, xsend, xrecv,
+def coupled(high, low, ref_h, ref_l):
+    size = high.shape[0]
+    main = dot_nn(jnp.concatenate([high, low], axis=0), ref_h[...])
+    return main[:size] + main[size:] + dot_nn(high, ref_l[...])
+
+
+def spread(value, matrix):
+    kmax = matrix.shape[0]
+    size = 2 * value.shape[0]
+    high, low = halves(jnp.concatenate([value[:, :kmax], value[:, kmax:]], axis=0))
+    parts = dot_nn(jnp.concatenate([high, low], axis=0), matrix)
+    return parts[:size] + parts[size:]
+
+
+def third_part(c, cr, sr, v, es1, g1h, g1l, cc, held):
+    size = CHUNKS[c]
+    kmax = es1.shape[0]
+    leafs = es1.shape[1] - kmax
+    at_f = pl.ds(sum(CHUNKS[:c]), size)
+    step = sr[c][0:1]
+    step = jnp.concatenate([step, step], axis=1)
+    high, low = halves(cr[at_f, :].astype(jnp.int32).astype(F32) * step)
+    pushed = coupled(high, low, g1h, g1l)
+    held[:size] = pushed
+    again = spread(pushed, es1[:, leafs:])
+    coarse = jnp.concatenate(
+        [v[0, at_f, :] - again[:size], v[1, at_f, :] - again[size:]], axis=1
+    )
+    high, low = halves(coarse)
+    main = dot_nn(jnp.concatenate([high, low], axis=0), cc[...])
+    total = held[:size] + (main[:size] + main[size:])
+    moved = spread(total, es1[:, :leafs])
+    return moved[:size], moved[size:]
+
+
+def solve_kernel(
+    inc, leaf, con, skel, rank_in, core,
+    out, cr, sr, v, es1, g1h, g1l, cc,
+    x, a, et, es0, g0h, g0l, va, idx, rank, cont, cq, ws, wr, cs, ss, held,
+    lsem, xsend, xrecv, csend, crecv, wsend, wrecv, ksend, krecv, ssend, srecv,
 ):
     fields, leafs = inc.shape[1], inc.shape[2]
     kmax = skel.shape[2]
     rows = leaf.shape[2]
-    box, me, box1, box2 = places()
-    right, left = (me + 1) % 4, (me + 3) % 4
+    box, me, box1, box2, box3 = places()
+    right, left, across = (me + 1) % 4, (me + 3) % 4, (me + 2) % 4
+    quad = box % 4
 
     def local(src, dst, at):
         copy = pltpu.make_async_copy(src, dst, lsem.at[at])
         copy.start()
         return copy
 
-    barrier = meet(((box, right), (box, left)))
+    barrier = meet(((box, right), (box, left), (box1, me), (box2, me), (box3, me)))
     load_idx = [
         local(skel.at[who], idx.at[at], at) for at, who in enumerate((box, box1, box2))
     ]
@@ -124,7 +163,8 @@
     load_con = local(con, cont, 4)
     load_x = local(inc, x, 5)
     load_a = local(leaf.at[0], a.at[me], 6)
-    pl.semaphore_wait(barrier, 2)
+    load_c = local(core, cq.at[quad], 7)
+    pl.semaphore_wait(barrier, 5)
 
     def ring(src, owner, part, at, to):
         return remote(src, a.at[owner, part], xsend.at[at], xrecv.at[at], (box, to))
@@ -133,6 +173,10 @@
     from_right_im = ring(leaf.at[0, 1], me, 1, 3, left)
     from_left_im = ring(leaf.at[0, 1], me, 1, 1, right)
     from_right_re = ring(leaf.at[0, 0], me, 0, 4, left)
+    cores = [
+        remote(core, cq.at[quad], csend.at[at], crecv.at[at], (who, me))
+        for at, who in enumerate((box1, box2, box3))
+    ]
 
     for copy in load_idx:
         copy.wait()
@@ -167,7 +211,7 @@
         et[block, rows:] = hit
         weight = weight + dot_nn(c_rows[:, block * rows : (block + 1) * rows], hit)
     weight = jnp.sum(weight, axis=0, keepdims=True)
-    weights[...] = jnp.broadcast_to(weight, weights.shape)
+    q0, q1 = weight[:, :kmax], weight[:, kmax:]
 
     def whole_block(owner, first):
         matrix = a[owner].reshape(2 * rows, leafs)
@@ -176,12 +220,12 @@
             at_f = pl.ds(start, size)
             y_re, y_im, picked = leaf_part(x, matrix, et[owner], at_f)
             at_cols = pl.ds(pl.multiple_of(owner * rows, rows), rows)
-            y[0, at_f, at_cols] = y_re
-            y[1, at_f, at_cols] = y_im
+            out[0, at_f, at_cols] = y_re
+            out[1, at_f, at_cols] = y_im
             if not first:
-                picked = picked + jnp.concatenate([v[0, at_f, :], v[1, at_f, :]], axis=0)
-            v[0, at_f, :] = picked[:size]
-            v[1, at_f, :] = picked[size:]
+                picked = picked + jnp.concatenate([va[0, at_f, :], va[1, at_f, :]], axis=0)
+            va[0, at_f, :] = picked[:size]
+            va[1, at_f, :] = picked[size:]
 
     load_x.wait()
     load_a.wait()
@@ -214,27 +258,15 @@
     put_complex(g1h, re_h, im_h)
     put_complex(g1l, re_l, im_l)
 
+    load_c.wait()
+    for copy in cores:
+        copy.wait_recv()
+    c_re = jnp.concatenate([cq[at, 0] for at in range(4)], axis=0)
+    c_im = jnp.concatenate([cq[at, 1] for at in range(4)], axis=0)
+    put_complex(cc, c_re, c_im)
+
     on_right.wait_recv()
     on_left.wait_recv()
-    for copy in (from_left_re, from_left_im, from_right_im, from_right_re, on_right, on_left):
-        copy.wait_send()
-
-
-def merge_kernel(
-    y, v_in, x, a, et, es0, es1, g0h, g0l, g1h, g1l, weights, core, out,
-    cq, cc, ws, wr, cs, cr, ss, sr, v, held,
-    lsem, csend, crecv, wsend, wrecv, ksend, krecv, ssend, srecv,
-):
-    leafs = y.shape[2]
-    kmax = cc.shape[0] // 2
-    rows = a.shape[2]
-    box, me, box1, box2 = places()
-    across = (me + 2) % 4
-    quad, quad2 = box % 4, box2 % 4
-    barrier = meet(((box1, me), (box2, me)))
-    load_c = pltpu.make_async_copy(core, cq.at[quad], lsem)
-    load_c.start()
-    q0, q1 = weights[0:1, :kmax], weights[0:1, kmax:]
     starts = [sum(CHUNKS[:c]) for c in range(len(CHUNKS))]
 
     def first_compute(c):
@@ -243,31 +275,18 @@
         matrix = a[across].reshape(2 * rows, leafs)
         y_re, y_im, picked = leaf_part(x, matrix, et[across], at_f)
         at_cols = pl.ds(pl.multiple_of(across * rows, rows), rows)
-        v_re = v_in[0, at_f, :] + picked[:size]
-        v_im = v_in[1, at_f, :] + picked[size:]
+        v_re = va[0, at_f, :] + picked[:size]
+        v_im = va[1, at_f, :] + picked[size:]
         v[0, at_f, :] = v_re[:, kmax:]
         v[1, at_f, :] = v_im[:, kmax:]
         value = jnp.concatenate([v_re[:, :kmax] * q0, v_im[:, :kmax] * q0], axis=1)
         ws[0, at_f, :], ws[1, at_f, :] = halves(value)
-        out[0, at_f, :] = y[0, at_f, :]
-        out[1, at_f, :] = y[1, at_f, :]
         out[0, at_f, at_cols] = y_re
         out[1, at_f, at_cols] = y_im
 
     def first_send(c):
         at_f = pl.ds(starts[c], CHUNKS[c])
         return remote(ws.at[:, at_f], wr.at[:, at_f], wsend.at[c], wrecv.at[c], (box1, me))
-
-    def coupled(high, low, ref_h, ref_l):
-        size = high.shape[0]
-        main = dot_nn(jnp.concatenate([high, low], axis=0), ref_h[...])
-        return main[:size] + main[size:] + dot_nn(high, ref_l[...])
-
-    def spread(value, matrix):
-        size = 2 * value.shape[0]
-        high, low = halves(jnp.concatenate([value[:, :kmax], value[:, kmax:]], axis=0))
-        parts = dot_nn(jnp.concatenate([high, low], axis=0), matrix)
-        return parts[:size] + parts[size:]
 
     def second_stage(c, arriving):
         size = CHUNKS[c]
@@ -291,57 +310,50 @@
         out[1, at_f, :] = out[1, at_f, :] - moved[size:, :leafs]
         return codes, steps
 
-    def third_stage(c, codes, steps):
-        size = CHUNKS[c]
-        at_f = pl.ds(starts[c], size)
-        codes.wait_recv()
-        steps.wait_recv()
-        step = sr[c][0:1]
-        step = jnp.concatenate([step, step], axis=1)
-        high, low = halves(cr[at_f, :].astype(jnp.int32).astype(F32) * step)
-        pushed = coupled(high, low, g1h, g1l)
-        held[:size] = pushed
-        again = spread(pushed, es1[:, leafs:])
-        coarse = jnp.concatenate(
-            [v[0, at_f, :] - again[:size], v[1, at_f, :] - again[size:]], axis=1
-        )
-        high, low = halves(coarse)
-        main = dot_nn(jnp.concatenate([high, low], axis=0), cc[...])
-        total = held[:size] + (main[:size] + main[size:])
-        moved = spread(total, es1[:, :leafs])
-        out[0, at_f, :] = out[0, at_f, :] - moved[:size]
-        out[1, at_f, :] = out[1, at_f, :] - moved[size:]
-
-    chunks = len(CHUNKS)
-    first_compute(0)
-    pl.semaphore_wait(barrier, 2)
-    sent = [first_send(0)]
-    core2 = remote(core, cq.at[quad], csend.at[0], crecv.at[0], (box2, me))
-    core1 = remote(core, cq.at[quad], csend.at[1], crecv.at[1], (box1, me))
-    codes = []
-    for c in range(1, chunks + 1):
-        if c < chunks:
+    def third_stage(c):
+        at_f = pl.ds(starts[c], CHUNKS[c])
+        codes[c][0].wait_recv()
+        codes[c][1].wait_recv()
+        m_re, m_im = third_part(c, cr, sr, v, es1, g1h, g1l, cc, held)
+        out[0, at_f, :] = out[0, at_f, :] - m_re
+        out[1, at_f, :] = out[1, at_f, :] - m_im
+
+    sent = {}
+    codes = {}
+    for c, late in ((0, False), (1, False), (0, True), (1, True), (2, False), (3, False), (2, True), (3, True)):
+        if late:
+            codes[c] = second_stage(c, sent[c])
+        else:
             first_compute(c)
-            sent.append(first_send(c))
-        codes.append(second_stage(c - 1, sent[c - 1]))
-        if c == 2:
-            core2.wait_recv()
-            core3 = remote(cq.at[quad2], cq.at[quad2], csend.at[2], crecv.at[2], (box1, me))
-
-    load_c.wait()
-    core1.wait_recv()
-    core3.wait_recv()
-    c_re = jnp.concatenate([cq[at, 0] for at in range(4)], axis=0)
-    c_im = jnp.concatenate([cq[at, 1] for at in range(4)], axis=0)
-    put_complex(cc, c_re, c_im)
-    for c in range(chunks):
-        third_stage(c, *codes[c])
-
-    for copy in [core1, core2, core3] + sent:
+            sent[c] = first_send(c)
+    last = len(CHUNKS) - 1
+    for c in range(last):
+        third_stage(c)
+    codes[last][0].wait_recv()
+    codes[last][1].wait_recv()
+
+    for copy in (from_left_re, from_left_im, from_right_im, from_right_re, on_right, on_left):
         copy.wait_send()
-    for pair in codes:
+    for copy in cores + list(sent.values()):
+        copy.wait_send()
+    for pair in codes.values():
         for copy in pair:
             copy.wait_send()
+
+
+def finish_kernel(y, cr, sr, v, es1, g1h, g1l, cc, out, held, done, sem):
+    last = len(CHUNKS) - 1
+    start, size = sum(CHUNKS[:last]), CHUNKS[last]
+    front, back = pl.ds(0, start), pl.ds(start, size)
+    early = pltpu.make_async_copy(y.at[:, front], out.at[:, front], sem.at[0])
+    early.start()
+    m_re, m_im = third_part(last, cr, sr, v, es1, g1h, g1l, cc, held)
+    done[0] = y[0, back, :] - m_re
+    done[1] = y[1, back, :] - m_im
+    rest = pltpu.make_async_copy(done, out.at[:, back], sem.at[1])
+    rest.start()
+    early.wait()
+    rest.wait()
 
 
 def body(incident, leaf_inverse, contrast, skel_index, ranks, top_core):
@@ -356,63 +368,66 @@
     hbm = pl.BlockSpec(memory_space=pltpu.HBM)
     made = [
         ((2, fields, leafs), F32),
-        ((2, fields, wide), F32),
-        ((2, fields, leafs), BF16),
-        ((4, 2, rows, leafs), BF16),
-        ((4, 2 * rows, wide), BF16),
-        ((kmax, leafs + kmax), BF16),
+        ((fields, wide), jnp.int16),
+        ((chunks, 8, kmax), F32),
+        ((2, fields, kmax), F32),
         ((kmax, leafs + kmax), BF16),
         ((wide, wide), BF16),
         ((wide, wide), BF16),
         ((wide, wide), BF16),
-        ((wide, wide), BF16),
-        ((8, wide), F32),
     ]
-
-    def in_hbm(value):
-        return pltpu.with_memory_space_constraint(value, pltpu.HBM)
-
+    operands = (
+        incident,
+        leaf_inverse,
+        contrast.reshape(1, leafs),
+        skel_index,
+        ranks.T,
+        jnp.swapaxes(top_core, 1, 2),
+    )
     state = pl.pallas_call(
-        gather_kernel,
+        solve_kernel,
         out_shape=[jax.ShapeDtypeStruct(*each) for each in made],
-        in_specs=[hbm] * 5,
+        in_specs=[hbm] * len(operands),
         out_specs=[vmem] * len(made),
         scratch_shapes=[
+            pltpu.VMEM((2, fields, leafs), BF16),
+            pltpu.VMEM((4, 2, rows, leafs), BF16),
+            pltpu.VMEM((4, 2 * rows, wide), BF16),
+            pltpu.VMEM((kmax, leafs + kmax), BF16),
+            pltpu.VMEM((wide, wide), BF16),
+            pltpu.VMEM((wide, wide), BF16),
+            pltpu.VMEM((2, fields, wide), F32),
             pltpu.VMEM((3, 2, kmax), jnp.int32),
             pltpu.VMEM((2, boxes), jnp.int32),
             pltpu.VMEM((1, leafs), F32),
-            dma((7,)), dma((6,)), dma((6,)),
-        ],
-        compiler_params=pltpu.CompilerParams(
-            collective_id=0, has_side_effects=True, vmem_limit_bytes=24 << 20
-        ),
-        name="gather",
-    )(*map(in_hbm, (incident, leaf_inverse, contrast.reshape(1, leafs), skel_index, ranks.T)))
-    return pl.pallas_call(
-        merge_kernel,
-        out_shape=jax.ShapeDtypeStruct(incident.shape, F32),
-        in_specs=[vmem] * len(made) + [hbm],
-        out_specs=vmem,
-        scratch_shapes=[
             pltpu.VMEM((4, 2, kq, kmax), BF16),
-            pltpu.VMEM((wide, wide), BF16),
             pltpu.VMEM((2, fields, wide), BF16),
             pltpu.VMEM((2, fields, wide), BF16),
             pltpu.VMEM((fields, wide), jnp.int16),
-            pltpu.VMEM((fields, wide), jnp.int16),
             pltpu.VMEM((chunks, 8, kmax), F32),
-            pltpu.VMEM((chunks, 8, kmax), F32),
-            pltpu.VMEM((2, fields, kmax), F32),
             pltpu.VMEM((max(CHUNKS), wide), F32),
-            dma, dma((3,)), dma((3,)),
+            dma((8,)), dma((6,)), dma((6,)), dma((3,)), dma((3,)),
             dma((chunks,)), dma((chunks,)), dma((chunks,)), dma((chunks,)),
             dma((chunks,)), dma((chunks,)),
         ],
         compiler_params=pltpu.CompilerParams(
-            collective_id=1, has_side_effects=True, vmem_limit_bytes=28 << 20
+            collective_id=0, has_side_effects=True, vmem_limit_bytes=32 << 20
         ),
-        name="merge",
-    )(*state, in_hbm(jnp.swapaxes(top_core, 1, 2)))
+        name="solve",
+    )(*(pltpu.with_memory_space_constraint(value, pltpu.HBM) for value in operands))
+    return pl.pallas_call(
+        finish_kernel,
+        out_shape=jax.ShapeDtypeStruct(incident.shape, F32),
+        in_specs=[vmem] * len(made),
+        out_specs=hbm,
+        scratch_shapes=[
+            pltpu.VMEM((CHUNKS[-1], wide), F32),
+            pltpu.VMEM((2, CHUNKS[-1], leafs), F32),
+            dma((2,)),
+        ],
+        compiler_params=pltpu.CompilerParams(vmem_limit_bytes=16 << 20),
+        name="finish",
+    )(*state)
 
 
 def solution(mesh):

time: 37.5 us -> 36.1 us (0.963)
  local copies, waits for them, and re-layouts: 1.32 us -> 0 us
    unnamed x1 -> x0, local copies, waits for them, and re-layouts: 1.32 us -> none
where the time goes in v5:
time: 36.1 us; the launch traced here: 36 us
  Pallas kernels  36 us (100%)
    pallas_call x1, Pallas kernels, body(): pl.pallas_call(solve_kernel, out_shape=[jax.ShapeDtypeStruct(*each) for e...  34.1 us
    pallas_call x1, Pallas kernels, body(): pl.pallas_call(finish_kernel, out_shape=jax.ShapeDtypeStruct(incident.sha...  1.9 us

profile of v5, /device:TPU:1, one launch (start us, length us, event | category | flops | bytes accessed | tf_op | source)
XLA Modules:
  0.0 36.0 jit_solution(5454796260267340685)
XLA Ops:
  0.0 34.1 %solve.1 = (f32[2,512,512]{2,1,0:T(8,128)S(1)}, s16[512,512]{1,0:T(8,128)(2,1)S(1)}, f32[4,8,256]{2,1,0:T(8,128)S(1)}, f32[2,512,256]{2,1,0:T(8,128)S(1)}, bf16[...) custom-call(bf16[2,512,512]{2,1,0:T(8,128)(2,1)} %inc.1, ...), custom_call_target="tpu_custom_call" | custom-call | tf_op jit(solution)/shard_map/solve/pallas_call | solution.py:387
  34.1 1.9 %finish.1 = f32[2,512,512]{2,1,0:T(8,128)} custom-call(f32[2,512,512]{2,1,0:T(8,128)S(1)} %get-tuple-element.13.y, s16[512,512]{1,0:T(8,128)(2,1)S(1)} %get-tuple-element.14.cr, f32[4,8,256]{2,1,0:T(8,128)S(1)} %get-tuple-element.15.sr, f32[2,512,256]{2,1,0:T(8,128)S(1)} %get-tuple-element.16.v, bf16[256,768]{1,0:T(8,128)(2,1)S(1)} %get-tuple-element.17.es1, ...), custom_call_target="tpu_custom_call" | custom-call | tf_op jit(solution)/shard_map/finish/pallas_call | solution.py:418

commit v6 on v5

--- a/solution.py
+++ b/solution.py
@@ -11,7 +11,7 @@
 WAVENUM = 0.7
 F32 = jnp.float32
 BF16 = jnp.bfloat16
-CHUNKS = (64, 160, 160, 128)
+CHUNKS = (64, 160, 192, 96)
 TOP = 32767.0
 
 
@@ -231,16 +231,16 @@
     load_a.wait()
     whole_block(me, True)
 
+    from_left_re.wait_recv()
+    on_right = ring(a.at[left, 0], left, 0, 2, right)
+    from_right_im.wait_recv()
+    on_left = ring(a.at[right, 1], right, 1, 5, left)
+
     g_re, g_im = green(columns[:, 2:3], own0, (8 * (box1 - box)).astype(F32))
     re_h, re_l = halves(g_re)
     im_h, im_l = halves(g_im)
     put_complex(g0h, re_h, im_h)
     put_complex(g0l, re_l, im_l)
-
-    from_left_re.wait_recv()
-    on_right = ring(a.at[left, 0], left, 0, 2, right)
-    from_right_im.wait_recv()
-    on_left = ring(a.at[right, 1], right, 1, 5, left)
 
     at_l = lax.broadcasted_iota(jnp.int32, (1, leafs), 1)
     lanes = jnp.concatenate([at_l, pick1_too], axis=1)
@@ -293,9 +293,12 @@
         at_f = pl.ds(starts[c], size)
         arriving.wait_recv()
         pushed = coupled(wr[0, at_f, :], wr[1, at_f, :], g0h, g0l)
-        moved = spread(pushed, es0[...])
-        v_re = v[0, at_f, :] - moved[:size, leafs:]
-        v_im = v[1, at_f, :] - moved[size:, leafs:]
+        high, low = halves(jnp.concatenate([pushed[:, :kmax], pushed[:, kmax:]], axis=0))
+        stacked = jnp.concatenate([high, low], axis=0)
+        parts = dot_nn(stacked, es0[:, leafs:])
+        moved = parts[: 2 * size] + parts[2 * size :]
+        v_re = v[0, at_f, :] - moved[:size]
+        v_im = v[1, at_f, :] - moved[size:]
         v[0, at_f, :] = v_re
         v[1, at_f, :] = v_im
         most = jnp.max(jnp.maximum(jnp.abs(v_re), jnp.abs(v_im)), axis=0, keepdims=True)
@@ -306,8 +309,10 @@
         ss[c] = jnp.broadcast_to(most * (1.0 / TOP) * q1, (8, kmax))
         codes = remote(cs.at[at_f], cr.at[at_f], ksend.at[c], krecv.at[c], (box2, me))
         steps = remote(ss.at[c], sr.at[c], ssend.at[c], srecv.at[c], (box2, me))
-        out[0, at_f, :] = out[0, at_f, :] - moved[:size, :leafs]
-        out[1, at_f, :] = out[1, at_f, :] - moved[size:, :leafs]
+        parts = dot_nn(stacked, es0[:, :leafs])
+        moved = parts[: 2 * size] + parts[2 * size :]
+        out[0, at_f, :] = out[0, at_f, :] - moved[:size]
+        out[1, at_f, :] = out[1, at_f, :] - moved[size:]
         return codes, steps
 
     def third_stage(c):

time: 36.1 us -> 36.5 us (1.011)
    pallas_call x1, Pallas kernels: 34.1 us -> 34.6 us  [body(): pl.pallas_call(solve_kernel, out_shape=[jax.ShapeDtypeStruct(*each) for e...]
where the time goes in v6:
time: 36.5 us; the launch traced here: 36.3 us
  Pallas kernels  36.3 us (99%)
    pallas_call x1, Pallas kernels, body(): pl.pallas_call(solve_kernel, out_shape=[jax.ShapeDtypeStruct(*each) for e...  34.6 us
    pallas_call x1, Pallas kernels, body(): pl.pallas_call(finish_kernel, out_shape=jax.ShapeDtypeStruct(incident.sha...  1.74 us

profile of v6, /device:TPU:1, one launch (start us, length us, event | category | flops | bytes accessed | tf_op | source)
XLA Modules:
  0.0 36.3 jit_solution(6550337559695378840)
XLA Ops:
  0.0 34.6 %solve.1 = (f32[2,512,512]{2,1,0:T(8,128)S(1)}, s16[512,512]{1,0:T(8,128)(2,1)S(1)}, f32[4,8,256]{2,1,0:T(8,128)S(1)}, f32[2,512,256]{2,1,0:T(8,128)S(1)}, bf16[...) custom-call(bf16[2,512,512]{2,1,0:T(8,128)(2,1)} %inc.1, ...), custom_call_target="tpu_custom_call" | custom-call | tf_op jit(solution)/shard_map/solve/pallas_call | solution.py:392
  34.6 1.7 %finish.1 = f32[2,512,512]{2,1,0:T(8,128)} custom-call(f32[2,512,512]{2,1,0:T(8,128)S(1)} %get-tuple-element.13.y, s16[512,512]{1,0:T(8,128)(2,1)S(1)} %get-tuple-element.14.cr, f32[4,8,256]{2,1,0:T(8,128)S(1)} %get-tuple-element.15.sr, f32[2,512,256]{2,1,0:T(8,128)S(1)} %get-tuple-element.16.v, bf16[256,768]{1,0:T(8,128)(2,1)S(1)} %get-tuple-element.17.es1, ...), custom_call_target="tpu_custom_call" | custom-call | tf_op jit(solution)/shard_map/finish/pallas_call | solution.py:423

commit v7 on v5

--- a/solution.py
+++ b/solution.py
@@ -11,7 +11,7 @@
 WAVENUM = 0.7
 F32 = jnp.float32
 BF16 = jnp.bfloat16
-CHUNKS = (64, 160, 160, 128)
+CHUNKS = (64, 160, 192, 96)
 TOP = 32767.0
 
 

time: 36.1 us -> 36 us (level)
  no operation moved by 1% of the time
where the time goes in v7:
time: 36 us; the launch traced here: 35.8 us
  Pallas kernels  35.8 us (99%)
    pallas_call x1, Pallas kernels, body(): pl.pallas_call(solve_kernel, out_shape=[jax.ShapeDtypeStruct(*each) for e...  34.1 us
    pallas_call x1, Pallas kernels, body(): pl.pallas_call(finish_kernel, out_shape=jax.ShapeDtypeStruct(incident.sha...  1.74 us

profile of v7, /device:TPU:1, one launch (start us, length us, event | category | flops | bytes accessed | tf_op | source)
XLA Modules:
  0.0 35.8 jit_solution(4986869313055940334)
XLA Ops:
  0.0 34.1 %solve.1 = (f32[2,512,512]{2,1,0:T(8,128)S(1)}, s16[512,512]{1,0:T(8,128)(2,1)S(1)}, f32[4,8,256]{2,1,0:T(8,128)S(1)}, f32[2,512,256]{2,1,0:T(8,128)S(1)}, bf16[...) custom-call(bf16[2,512,512]{2,1,0:T(8,128)(2,1)} %inc.1, ...), custom_call_target="tpu_custom_call" | custom-call | tf_op jit(solution)/shard_map/solve/pallas_call | solution.py:387
  34.1 1.7 %finish.1 = f32[2,512,512]{2,1,0:T(8,128)} custom-call(f32[2,512,512]{2,1,0:T(8,128)S(1)} %get-tuple-element.13.y, s16[512,512]{1,0:T(8,128)(2,1)S(1)} %get-tuple-element.14.cr, f32[4,8,256]{2,1,0:T(8,128)S(1)} %get-tuple-element.15.sr, f32[2,512,256]{2,1,0:T(8,128)S(1)} %get-tuple-element.16.v, bf16[256,768]{1,0:T(8,128)(2,1)S(1)} %get-tuple-element.17.es1, ...), custom_call_target="tpu_custom_call" | custom-call | tf_op jit(solution)/shard_map/finish/pallas_call | solution.py:418
